TPU v7x, 512 devices: a whole 4x8x8 slice. The times are simulated.
512 devices in a mesh: lat: 64 (over y_lo, x, z), lon: 8 (over y_hi, core).
Axes of the slice: x: 4, y: 8 (y_hi: 4, y_lo: 2; y = y_hi * 2 + y_lo), z: 8, core: 2. Of those that a mesh axis runs over, the one named last changes fastest.
Arguments:
- coefficients: float32 [256, 2, 3, 2, 513], P('lat'), may hold values from -0.03125 to 0.03125
- pair_orders: int32 [256], replicated, may hold values from 0 to 255, each once
Outputs:
- potential: float32 [3, 2, 1024, 2048], P(None, None, 'lat', 'lon')
- magnetic_field: float32 [3, 2, 1024, 2048], P(None, None, 'lat', 'lon')
Inputs may be any that keep to these rules, and one draw needn't show every extreme that they name: A permutation of 0 to 255; row p of coefficients holds the orders pair_orders[p] and 511 - pair_orders[p].
All inputs are finite; a program needn't handle non-finite values.
Results may differ from a plain program's by a relative error of at most 0.0003.
Values sent between devices are 32-bit elements; how exact they have to be, the bound alone decides.
No kernel may reach another device: no remote copies, remote signals or barrier semaphores. Data moves between devices by JAX's collectives and lax.ppermute only.
A program may use at most 64 MiB of HBM per device.

v0:
```python
import math

import jax
import jax.numpy as jnp
from jax import lax
from jax.sharding import PartitionSpec as P

NT = 1024
NP = 2048
STEPS = 2


soft_floor = 1.0
resist = 0.2
time_step = 0.3
rescale_at = 10000000000.0
block_steps = 128
span_start = math.pi / 6.0
span_width = 2.0 * math.pi / 3.0


def with_halo(value, sides, width, wrap):
    for axis, dim in sides:
        size, length = (lax.axis_size(axis), value.shape[dim])
        up = [(i, (i + 1) % size) for i in range(size if wrap else size - 1)]
        down = [(j, i) for i, j in up]
        last = lax.slice_in_dim(value, length - width, length, axis=dim)
        first = lax.slice_in_dim(value, 0, width, axis=dim)
        before = lax.ppermute(last, axis, up)
        after = lax.ppermute(first, axis, down)
        value = jnp.concatenate([before, value, after], axis=dim)
    return value


def row_angles(row_ids, row_total):
    return span_start + (row_ids.astype(jnp.float32) + 0.5) * (span_width / row_total)


def norm_logs(order_total):
    degrees = jnp.arange(1, order_total, dtype=jnp.float32)
    log_terms = 0.5 * jnp.log((2.0 * degrees + 1.0) / (2.0 * degrees))
    return jnp.concatenate([jnp.zeros((1,), jnp.float32), jnp.cumsum(log_terms)]) - 0.5 * jnp.log(
        4.0 * math.pi
    )


def pick_logs(log_table, orders):
    order_grid = jnp.arange(log_table.shape[0], dtype=jnp.int32)
    return jnp.sum(
        jnp.where(order_grid[None, :] == orders[:, None], log_table[None, :], 0.0), axis=1
    )


def synthesize(coef_rows, small_orders, angles, order_total):
    pair_count = coef_rows.shape[0]
    columns = coef_rows.shape[1] * coef_rows.shape[2] * coef_rows.shape[3]
    packed = coef_rows.shape[4]
    block_count = -(-packed // block_steps)
    padded = block_count * block_steps
    flat_coef = jnp.pad(
        coef_rows.reshape(pair_count, columns, packed), ((0, 0), (0, 0), (0, padded - packed))
    )
    large_orders = order_total - 1 - small_orders
    low_order = small_orders.astype(jnp.float32)
    high_order = large_orders.astype(jnp.float32)
    switch = order_total - low_order
    positions = jnp.arange(padded, dtype=jnp.float32)
    low_mask = (positions[None, :] < switch[:, None]).astype(jnp.float32)
    masked = flat_coef[:, None, :, :] * jnp.stack([low_mask, 1.0 - low_mask], axis=1)[:, :, None, :]
    log_table = norm_logs(order_total)
    log_sin = jnp.log(jnp.sin(angles))
    cosine = jnp.cos(angles)
    seed_low = pick_logs(log_table, small_orders)[:, None] + low_order[:, None] * log_sin[None, :]
    seed_high = pick_logs(log_table, large_orders)[:, None] + high_order[:, None] * log_sin[None, :]
    log_big = math.log(rescale_at)

    def advance(carried, step_now):
        previous, current, scaling = carried
        low_side = step_now < switch
        order_now = jnp.where(low_side, low_order, high_order)
        degree = jnp.where(low_side, low_order + step_now, step_now - 1.0)
        starting = (degree == order_now)[:, None]
        factor = jnp.sqrt(
            jnp.maximum(4.0 * degree * degree - 1.0, 1.0)
            / jnp.maximum(degree * degree - order_now * order_now, 1.0)
        )
        prior_degree = degree - 1.0
        back_factor = jnp.where(
            prior_degree > order_now,
            jnp.sqrt(
                (prior_degree * prior_degree - order_now * order_now)
                / jnp.maximum(4.0 * prior_degree * prior_degree - 1.0, 1.0)
            ),
            0.0,
        )
        next_value = factor[:, None] * (cosine[None, :] * current - back_factor[:, None] * previous)
        seed_now = jnp.where(low_side[:, None], seed_low, seed_high)
        previous = jnp.where(starting, 0.0, current)
        current = jnp.where(starting, 1.0, next_value)
        scaling = jnp.where(starting, seed_now, scaling)
        too_big = jnp.abs(current) > rescale_at
        shrink = jnp.where(too_big, 1.0 / rescale_at, 1.0)
        previous = previous * shrink
        current = current * shrink
        scaling = scaling + jnp.where(too_big, log_big, 0.0)
        return ((previous, current, scaling), current * jnp.exp(scaling))

    def run_block(carried, block_index):
        rec_state, synth_sum = carried
        step_values = block_index.astype(jnp.float32) * block_steps + jnp.arange(
            block_steps, dtype=jnp.float32
        )
        rec_state, values = lax.scan(advance, rec_state, step_values, unroll=8)
        coef_block = lax.dynamic_slice_in_dim(masked, block_index * block_steps, block_steps, 3)
        synth_sum = synth_sum + jnp.einsum(
            "spt,pkcs->pkct",
            values,
            coef_block,
            precision=lax.Precision.HIGHEST,
            preferred_element_type=jnp.float32,
        )
        return ((rec_state, synth_sum), None)

    zero_rows = jnp.zeros((pair_count, angles.shape[0]), jnp.float32)
    zero_sum = jnp.zeros((pair_count, 2, columns, angles.shape[0]), jnp.float32)
    scanned = lax.scan(
        run_block,
        ((zero_rows, zero_rows, zero_rows), zero_sum),
        jnp.arange(block_count, dtype=jnp.int32),
    )
    synth_sum = scanned[0][1]
    return synth_sum.reshape(pair_count * 2, 2, columns // 2, angles.shape[0])


def sector_table(slot_orders, column_start, col_count, point_total):
    column_ids = column_start + jnp.arange(col_count, dtype=jnp.int32)
    turn_count = slot_orders[:, None] * column_ids[None, :] % point_total
    phase_angle = turn_count.astype(jnp.float32) * (2.0 * math.pi / point_total)
    return jnp.stack([jnp.cos(phase_angle), jnp.sin(phase_angle)], axis=1)


def transform(rows_part, sector_basis):
    return jnp.einsum(
        "gxcr,gxf->crf",
        rows_part,
        sector_basis,
        precision=lax.Precision.HIGHEST,
        preferred_element_type=jnp.float32,
    )


def curl(padded, row_sin, phi_ratio):
    center = padded[:, :, 1:-1, 1:-1]
    theta_diff = 0.5 * (padded[:, :, 2:, 1:-1] - padded[:, :, :-2, 1:-1])
    phi_scale = (1.0 / (2.0 * phi_ratio * row_sin))[None, :, None]
    lifted = jnp.pad(center, ((0, 0), (1, 1), (0, 0), (0, 0)))
    radial_diff = 0.5 * (lifted[:, 2:] - lifted[:, :-2])
    phi_radial = (padded[0, :, 1:-1, 2:] - padded[0, :, 1:-1, :-2]) * phi_scale
    phi_theta = (padded[1, :, 1:-1, 2:] - padded[1, :, 1:-1, :-2]) * phi_scale
    return jnp.stack(
        [theta_diff[2] - phi_theta, phi_radial - radial_diff[2], radial_diff[1] - theta_diff[0]]
    )


def cross_product(first_vec, second_vec):
    return jnp.stack(
        [
            first_vec[1] * second_vec[2] - first_vec[2] * second_vec[1],
            first_vec[2] * second_vec[0] - first_vec[0] * second_vec[2],
            first_vec[0] * second_vec[1] - first_vec[1] * second_vec[0],
        ]
    )


def drift(magnetic, current):
    lorentz = cross_product(current, magnetic)
    velocity = lorentz / (jnp.sum(magnetic * magnetic, axis=0) + soft_floor)
    return cross_product(velocity, magnetic) - resist * current


def per_device(coefficients, pair_orders):
    lat_count = lax.axis_size("lat")
    lon_count = lax.axis_size("lon")
    lat_pos = lax.axis_index("lat")
    lon_pos = lax.axis_index("lon")
    pair_local = coefficients.shape[0]
    levels = coefficients.shape[3]
    order_total = 2 * pair_orders.shape[0]
    row_total = NT
    point_total = NP
    band_rows = row_total // lat_count
    sector_cols = point_total // lon_count
    own_pairs = lax.dynamic_slice_in_dim(pair_orders, lat_pos * pair_local, pair_local)
    slot_orders = jnp.stack([pair_orders, order_total - 1 - pair_orders], axis=1).reshape(
        order_total
    )
    own_table = sector_table(slot_orders, lon_pos * sector_cols, sector_cols, point_total)
    angles = row_angles(jnp.arange(row_total, dtype=jnp.int32), row_total)
    spectral = synthesize(coefficients, own_pairs, angles, order_total)
    synth_grid = transform(
        lax.all_to_all(spectral, "lat", split_axis=3, concat_axis=0, tiled=True), own_table
    )
    potential = synth_grid.reshape(3, levels, band_rows, sector_cols)
    global_rows = lat_pos * band_rows + jnp.arange(-2, band_rows + 2, dtype=jnp.int32)
    sin_all = jnp.sin(row_angles(global_rows, row_total))
    sin_inner = sin_all[2:-2]
    phi_ratio = 3.0 * row_total / point_total
    magnetic = potential

    def extend_rims(values):
        taller = with_halo(values, (("lat", 2),), 1, False)
        return with_halo(taller, (("lon", 3),), 1, True)

    for step_now in range(STEPS):
        magnetic = curl(extend_rims(potential), sin_inner, phi_ratio)
        current = curl(extend_rims(magnetic), sin_inner, phi_ratio)
        potential = potential + time_step * drift(magnetic, current)
    return (potential, magnetic)


def solution(mesh):
    in_specs = (P("lat", None, None, None, None), P())
    out_specs = (P(None, None, "lat", "lon"), P(None, None, "lat", "lon"))
    return jax.shard_map(
        per_device, mesh=mesh, in_specs=in_specs, out_specs=out_specs, check_vma=False
    )
```

profile of v0, /device:TPU:40, one launch (start us, length us, event | category | flops | bytes accessed | tf_op | source)
XLA Modules:
  0.0 1125.7 jit_solution(11292824940193635866)
XLA Ops:
  3.7 957.0 %while.59 = (s32[]{:T(128)}, f32[4,1024]{1,0:T(4,128)S(1)}, f32[4,1024]{1,0:T(4,128)S(1)}, f32[4,1024]{1,0:T(4,128)S(1)}, f32[4,2,12,1024]{3,2,1,0:T(8,128)S(1)}...) while((s32[]{:T(128)}, f32[4,1024]{1,0:T(4,128)S(1)}, ...), condition=%wide.region_7.8_spmd.clone.clone.clone.clone, body=%wide.region_4.7_spmd.clone.clone.clone.clone.sunk | while | flops 152044704 | bytes 4487110 | solution.py:126
  5.0 187.1 %while.60 = (s32[]{:T(128)}, f32[4,1024]{1,0:T(4,128)S(1)}, f32[4,1024]{1,0:T(4,128)S(1)}, f32[4,1024]{1,0:T(4,128)S(1)}, f32[16,8,4,1024]{3,2,1,0:T(4,128)S(1)}...) while((s32[]{:T(128)}, f32[4,1024]{1,0:T(4,128)S(1)}, ...), condition=%wide.region_6.6_spmd.clone, body=%wide.region_5.5_spmd.clone.sunk | while | flops 832281 | bytes 1364985 | solution.py:113
  196.4 187.1 %while.60 = (s32[]{:T(128)}, f32[4,1024]{1,0:T(4,128)S(1)}, f32[4,1024]{1,0:T(4,128)S(1)}, f32[4,1024]{1,0:T(4,128)S(1)}, f32[16,8,4,1024]{3,2,1,0:T(4,128)S(1)}...) while((s32[]{:T(128)}, f32[4,1024]{1,0:T(4,128)S(1)}, ...), condition=%wide.region_6.6_spmd.clone, body=%wide.region_5.5_spmd.clone.sunk | while | flops 832281 | bytes 1364985 | solution.py:113
  387.8 187.1 %while.60 = (s32[]{:T(128)}, f32[4,1024]{1,0:T(4,128)S(1)}, f32[4,1024]{1,0:T(4,128)S(1)}, f32[4,1024]{1,0:T(4,128)S(1)}, f32[16,8,4,1024]{3,2,1,0:T(4,128)S(1)}...) while((s32[]{:T(128)}, f32[4,1024]{1,0:T(4,128)S(1)}, ...), condition=%wide.region_6.6_spmd.clone, body=%wide.region_5.5_spmd.clone.sunk | while | flops 832281 | bytes 1364985 | solution.py:113
  579.2 187.1 %while.60 = (s32[]{:T(128)}, f32[4,1024]{1,0:T(4,128)S(1)}, f32[4,1024]{1,0:T(4,128)S(1)}, f32[4,1024]{1,0:T(4,128)S(1)}, f32[16,8,4,1024]{3,2,1,0:T(4,128)S(1)}...) while((s32[]{:T(128)}, f32[4,1024]{1,0:T(4,128)S(1)}, ...), condition=%wide.region_6.6_spmd.clone, body=%wide.region_5.5_spmd.clone.sunk | while | flops 832281 | bytes 1364985 | solution.py:113
  770.6 187.1 %while.60 = (s32[]{:T(128)}, f32[4,1024]{1,0:T(4,128)S(1)}, f32[4,1024]{1,0:T(4,128)S(1)}, f32[4,1024]{1,0:T(4,128)S(1)}, f32[16,8,4,1024]{3,2,1,0:T(4,128)S(1)}...) while((s32[]{:T(128)}, f32[4,1024]{1,0:T(4,128)S(1)}, ...), condition=%wide.region_6.6_spmd.clone, body=%wide.region_5.5_spmd.clone.sunk | while | flops 832281 | bytes 1364985 | solution.py:113
  960.7 5.0 copy.35
  965.8 10.7 reshape.753
  976.5 14.9 %all-to-all-start = ((f32[64,1,1536]{2,1,0:T(1,128)}), f32[64,1,1536]{2,1,0:T(1,128)S(1)}, u32[]{:S(2)}, u32[]{:S(2)}) async-start(f32[64,1,1536]{2,1,0:T(1,128)} %reshape.753), calls=%async_computation | async-start | bytes 786432 | tf_op jit(solution)/shard_map/all_to_all | solution.py:201
  991.8 3.2 fusion.103
  995.0 12.2 %all-to-all-done = f32[64,1,1536]{2,1,0:T(1,128)S(1)} async-done(((f32[64,1,1536]{2,1,0:T(1,128)}), f32[64,1,1536]{2,1,0:T(1,128)S(1)}, u32[]{:S(2)}, u32[]{:S(2)}) %all-to-all-start) | async-done | bytes 393248 | tf_op jit(solution)/shard_map/all_to_all | solution.py:201
  1009.3 11.3 %reshape.754 = f32[1024,6,2,8]{3,2,1,0:T(2,128)} reshape(f32[64,1536]{1,0:T(8,128)S(1)} %reduce.2) | data formatting | bytes 786432
  1020.6 7.3 copy.46
  1030.8 3.2 collective-permute-start
  1034.1 2.6 collective-permute-start.1
  1036.8 7.0 collective-permute-done.1
  1048.3 5.3 collective-permute-done.3
  1055.7 8.1 collective-permute-start.5
  1069.7 5.3 collective-permute-done.7
  1075.4 8.4 collective-permute-start.8
  1085.7 7.8 collective-permute-done.9
  1098.0 5.3 collective-permute-done.11
  1105.4 8.1 collective-permute-start.13
  1119.4 5.3 collective-permute-done.15
  (1890 shorter events, 584.0 us)
Async XLA Ops:
  965.8 25.6 %copy-start.1 = (s32[256]{0:T(256)S(1)}, s32[256]{0:T(256)}, u32[]{:S(2)}) copy-start(s32[256]{0:T(256)} %param.7) | copy-start | bytes 3076
  976.5 30.7 %all-to-all-start = ((f32[64,1,1536]{2,1,0:T(1,128)}), f32[64,1,1536]{2,1,0:T(1,128)S(1)}, u32[]{:S(2)}, u32[]{:S(2)}) async-start(f32[64,1,1536]{2,1,0:T(1,128)} %reshape.753), calls=%async_computation | async-start | bytes 786432 | tf_op jit(solution)/shard_map/all_to_all | solution.py:201
  1030.8 5.9 collective-permute-start
  1034.1 9.7 collective-permute-start.1
  1043.9 4.4 collective-permute-start.2
  1045.8 7.8 collective-permute-start.3
  1053.8 10.1 collective-permute-start.4
  1055.7 9.5 collective-permute-start.5
  1065.3 4.4 collective-permute-start.6
  1067.2 7.8 collective-permute-start.7
  1075.4 10.3 collective-permute-start.8
  1083.8 9.7 collective-permute-start.9
  1093.6 4.4 collective-permute-start.10
  1095.5 7.8 collective-permute-start.11
  1103.5 22.2 %copy-start = (f32[3,2,16,256]{3,2,1,0:T(8,128)}, f32[3,2,16,256]{3,2,1,0:T(8,128)S(1)}, u32[]{:S(2)}) copy-start(f32[3,2,16,256]{3,2,1,0:T(8,128)S(1)} %get-tuple-element.812) | copy-start | bytes 294916
  1103.5 10.1 collective-permute-start.12
  1105.4 9.5 collective-permute-start.13
  1115.0 4.4 collective-permute-start.14
  1117.0 7.8 collective-permute-start.15
where the time goes:
time: 1140 us; the launch traced here: 1130 us
  other arithmetic  486 us (43%)
  loops' own time  409 us (36%)
  local copies, waits for them, and re-layouts  96.7 us (8%)
  starting transfers between devices  68.5 us (6%)
  waiting for transfers between devices  50.8 us (4%)
  matrix products  13.7 us (1%)
    another operation x5, loops' own time, run_block(): rec_state, values = lax.scan(advance, rec_state, step_values, unroll=8)  403 us
    sqrt x240, other arithmetic, advance(): jnp.sqrt(jnp.maximum(4.0 * degree * degree - 1.0, 1.0) / jnp.maximum(degr...  204 us
    eq x400, other arithmetic, advance(): starting = (degree == order_now)[:, None]  197 us
    while x560, other arithmetic  57.7 us
    slice x80, local copies, waits for them, and re-layouts, run_block(): rec_state, values = lax.scan(advance, rec_state, step_values, unroll=8)  48.3 us
    ppermute x8, waiting for transfers between devices, with_halo(): before = lax.ppermute(last, axis, up)  36 us
    ppermute x8, starting transfers between devices, with_halo(): after = lax.ppermute(first, axis, down)  35.6 us
    unnamed x8, local copies, waits for them, and re-layouts  23 us
  transfers between devices with their start and end apart: 17, of which 9 were waited for; matrix products, arithmetic and copies ran while one was open for 0% of the time, Pallas kernels for 0%

commit v1 on v0

v1 whole, which is shorter than its diff:
```python
import math

import jax
import jax.numpy as jnp
import numpy as np
from jax import lax
from jax.experimental import pallas as pl
from jax.experimental.pallas import tpu as pltpu
from jax.sharding import PartitionSpec as P

ORDERS = 512
NT = 1024
NP = 2048
STEPS = 2
LAT = 64
LON = 8
BAND = NT // LAT
SECTOR = NP // LON
HALO = 4
EXT = BAND + 2 * HALO
PAIRS_LOCAL = 4
HALF = LAT // 2
CHUNKS = 18
COLS = SECTOR + 16

soft_floor = 1.0
resist = 0.2
time_step = 0.3
rescale_at = 1.0e10
block_steps = 16
span_start = math.pi / 6.0
span_width = 2.0 * math.pi / 3.0

EXCHANGE = list(range(HALF)) + [LAT - 1 - u for u in range(HALF)]


def geometry():
    rows = (
        BAND * np.arange(HALF)[None, None, :]
        + 8 * np.arange(2)[:, None, None]
        + np.arange(8)[None, :, None]
    )
    theta = span_start + (rows + 0.5) * (span_width / NT)
    cosine = np.tile(np.cos(theta), (1, 1, PAIRS_LOCAL))
    log_sin = np.tile(np.log(np.sin(theta)), (1, 1, PAIRS_LOCAL))
    return np.concatenate([cosine, log_sin]).astype(np.float32)


def norm_logs():
    k = np.arange(1, ORDERS, dtype=np.float64)
    logs = np.concatenate([[0.0], np.cumsum(0.5 * np.log((2 * k + 1) / (2 * k)))])
    return (logs - 0.5 * np.log(4 * np.pi)).astype(np.float32)


def split2(value):
    high = value.astype(jnp.bfloat16)
    low = (value - high.astype(jnp.float32)).astype(jnp.bfloat16)
    return high, low


def dot(a, b):
    return jnp.dot(a, b, preferred_element_type=jnp.float32)


def synth_kernel(
    order_ref, log_ref, geom_ref, coef_ref, out_ref,
    fac_ref, back_ref, leg_ref, coefs_ref, wh_ref, wl_ref, stack_ref, extra_ref,
):
    lane = lax.broadcasted_iota(jnp.int32, (8, 128), 1)
    pair_of_lane = lane // HALF
    unit = lane % HALF

    def per_pair(values):
        result = jnp.full((8, 128), values[0], values[0].dtype)
        for p in range(1, PAIRS_LOCAL):
            result = jnp.where(pair_of_lane == p, values[p], result)
        return result

    lows = [order_ref[p] for p in range(PAIRS_LOCAL)]
    low = per_pair([o.astype(jnp.float32) for o in lows])
    high = (ORDERS - 1.0) - low
    switch = ORDERS - low

    def factors(c, _):
        base = c * 8
        step = lax.broadcasted_iota(jnp.int32, (8, 128), 0).astype(jnp.float32) + base.astype(jnp.float32)
        low_side = step < switch
        order = jnp.where(low_side, low, high)
        degree = jnp.where(low_side, low + step, step - 1.0)
        prior = degree - 1.0
        order2 = order * order
        degree2 = degree * degree
        prior2 = prior * prior
        factor = jnp.sqrt(jnp.maximum(4.0 * degree2 - 1.0, 1.0) / jnp.maximum(degree2 - order2, 1.0))
        back = jnp.sqrt(jnp.maximum(prior2 - order2, 0.0) / jnp.maximum(4.0 * prior2 - 1.0, 1.0))
        fac_ref[pl.ds(pl.multiple_of(base, 8), 8), :] = factor
        back_ref[pl.ds(pl.multiple_of(base, 8), 8), :] = jnp.where(prior > order, factor * back, 0.0)
        return 0

    lax.fori_loop(0, 65, factors, 0)

    coefs_ref[...] = jnp.zeros_like(coefs_ref)
    for p in range(PAIRS_LOCAL):
        for x in range(2):
            for c in range(3):
                row = (p * 2 + x) * 8 + c * 2
                coefs_ref[row:row + 2, 0:513] = coef_ref[p, x, c]
    slot = lax.broadcasted_iota(jnp.int32, (8, 512), 1)
    for p in range(PAIRS_LOCAL):
        is_low = slot < ORDERS - lows[p]
        low_sign = 1.0 - 2.0 * (slot % 2).astype(jnp.float32)
        high_sign = 1.0 - 2.0 * ((slot + lows[p]) % 2).astype(jnp.float32)
        for x in range(2):
            row = (p * 2 + x) * 8
            both = coefs_ref[row:row + 8, 0:512]
            parts = [jnp.where(is_low, both, 0.0), jnp.where(is_low, 0.0, both)]
            for side in range(2):
                for h in range(2):
                    w = parts[h] if side == 0 else parts[h] * (low_sign if h == 0 else high_sign)
                    at = (((side * PAIRS_LOCAL + p) * 2 + h) * 2 + x) * 8
                    wh, wl = split2(w)
                    wh_ref[at:at + 8, :] = wh.astype(jnp.float32)
                    wl_ref[at:at + 8, :] = wl.astype(jnp.float32)

    cosine = [geom_ref[0], geom_ref[1]]
    log_sin = [geom_ref[2], geom_ref[3]]
    norm_low = per_pair([log_ref[o] for o in lows])
    norm_high = per_pair([log_ref[ORDERS - 1 - o] for o in lows])
    seed_low = [norm_low + low * log_sin[v] for v in range(2)]
    seed_high = [norm_high + high * log_sin[v] for v in range(2)]
    start_scale = [jnp.exp(seed_high[v]) for v in range(2)]
    log_big = math.log(rescale_at)

    def run(base, count, state, restart, first):
        state = [list(s) for s in state]
        for k in range(count):
            s = base + k
            fac = fac_ref[pl.ds(s, 1), :]
            back = back_ref[pl.ds(s, 1), :]
            if restart:
                starting = switch == (s.astype(jnp.float32) if not isinstance(s, int) else float(s))
            for v in range(2):
                previous, current, scaling, scale = state[v]
                if first and k == 0:
                    value = jnp.ones((8, 128), jnp.float32)
                else:
                    value = (fac * cosine[v]) * current - back * previous
                if restart:
                    value = jnp.where(starting, 1.0, value)
                    scaling = jnp.where(starting, seed_high[v], scaling)
                    scale = jnp.where(starting, start_scale[v], scale)
                state[v] = [current, value, scaling, scale]
                at = s * 8 if isinstance(s, int) else pl.multiple_of(s * 8, 8)
                leg_ref[v, pl.ds(at, 8), :] = value * scale
        for v in range(2):
            previous, current, scaling, scale = state[v]
            big = jnp.abs(current) > rescale_at
            shrink = jnp.where(big, 1.0 / rescale_at, 1.0)
            scaling = scaling + jnp.where(big, log_big, 0.0)
            state[v] = [previous * shrink, current * shrink, scaling, jnp.exp(scaling)]
        return tuple(tuple(s) for s in state)

    zero = jnp.zeros((8, 128), jnp.float32)
    state = tuple((zero, zero, seed_low[v], jnp.exp(seed_low[v])) for v in range(2))
    state = run(0, block_steps, state, False, True)
    state = lax.fori_loop(
        1, 16, lambda b, st: run(b * block_steps, block_steps, st, False, False), state
    )
    state = lax.fori_loop(
        16, 32, lambda b, st: run(b * block_steps, block_steps, st, True, False), state
    )
    run(512, 1, state, True, False)

    tail_sign = per_pair([1.0 - 2.0 * (o % 2).astype(jnp.float32) for o in lows])
    tails = []
    for x in range(2):
        tail = jnp.zeros((8, 128), jnp.float32)
        for p in range(PAIRS_LOCAL):
            row = (p * 2 + x) * 8
            column = jnp.broadcast_to(coefs_ref[row:row + 8, 512:513], (8, 128))
            tail = jnp.where(pair_of_lane == p, column, tail)
        tails.append(tail)
    wh = wh_ref[...].astype(jnp.bfloat16)
    wl = wl_ref[...].astype(jnp.bfloat16)
    for v in range(2):
        for t in range(0, 8, 2):
            values = jnp.concatenate(
                [leg_ref[v, pl.ds(t + d, 512, stride=8), :] for d in range(2)], axis=1
            )
            vh, vl = split2(values)
            summed = dot(wh, vh) + dot(wl, vh) + dot(wh, vl)
            for d in range(2):
                r = 8 * v + t + d
                last = leg_ref[v, pl.ds(512 * 8 + t + d, 1), :]
                part = summed[:, 128 * d:128 * d + 128]
                for side in range(2):
                    for h in range(2):
                        for x in range(2):
                            picked = None
                            for p in range(PAIRS_LOCAL):
                                at = (((side * PAIRS_LOCAL + p) * 2 + h) * 2 + x) * 8
                                block = part[at:at + 8, :]
                                picked = block if p == 0 else jnp.where(pair_of_lane == p, block, picked)
                            if h == 1:
                                term = tails[x] * last
                                picked = picked + (term if side == 0 else term * tail_sign)
                            e = HALO + (r if side == 0 else BAND - 1 - r)
                            stack_ref[(side * 2 + h) * 2 + x, 6 * e:6 * e + 6, :] = picked[0:6]

    wide_unit = lax.broadcasted_iota(jnp.int32, (24, 128), 1) % HALF
    for h in range(2):
        for x in range(2):
            north, south = h * 2 + x, 4 + h * 2 + x
            n_first, n_last = stack_ref[north, 24:48, :], stack_ref[north, 96:120, :]
            s_first, s_last = stack_ref[south, 24:48, :], stack_ref[south, 96:120, :]
            stack_ref[north, 0:24, :] = jnp.where(wide_unit == 0, 0.0, pltpu.roll(n_last, 1, 1))
            stack_ref[north, 120:144, :] = jnp.where(
                wide_unit == HALF - 1, s_first, pltpu.roll(n_first, 127, 1)
            )
            stack_ref[south, 0:24, :] = jnp.where(
                wide_unit == HALF - 1, n_last, pltpu.roll(s_last, 127, 1)
            )
            stack_ref[south, 120:144, :] = jnp.where(wide_unit == 0, 0.0, pltpu.roll(s_first, 1, 1))

    wide_lane = lax.broadcasted_iota(jnp.int32, (HALF, 128), 1)
    for side in range(2):
        for h in range(2):
            for x in range(2):
                which = (side * 2 + h) * 2 + x
                turned = stack_ref[which, 0:128, :].T
                for p in range(PAIRS_LOCAL):
                    chunk = (p * 2 + h) * 2 + x
                    out_ref[pl.ds(side * HALF * CHUNKS + chunk, HALF, stride=CHUNKS), :] = turned[
                        HALF * p:HALF * p + HALF, :
                    ]
                for copy in range(2):
                    at = copy * 64 + (h * 2 + x) * 16
                    extra_ref[at:at + 16, :] = stack_ref[which, 128:144, :]
        turned = extra_ref[...].T
        for q in range(2):
            first = turned[2 * q * HALF:2 * q * HALF + HALF, :]
            second = turned[(2 * q + 1) * HALF:(2 * q + 2) * HALF, :]
            out_ref[pl.ds(side * HALF * CHUNKS + 16 + q, HALF, stride=CHUNKS), :] = jnp.where(
                wide_lane < 64, first, second
            )


def synthesize(own_orders, coefficients):
    scratch = [
        pltpu.VMEM((520, 128), jnp.float32),
        pltpu.VMEM((520, 128), jnp.float32),
        pltpu.VMEM((2, 520 * 8, 128), jnp.float32),
        pltpu.VMEM((64, 640), jnp.float32),
        pltpu.VMEM((256, 512), jnp.float32),
        pltpu.VMEM((256, 512), jnp.float32),
        pltpu.VMEM((8, 144, 128), jnp.float32),
        pltpu.VMEM((128, 128), jnp.float32),
    ]
    return pl.pallas_call(
        synth_kernel,
        out_shape=jax.ShapeDtypeStruct((LAT * CHUNKS, 128), jnp.float32),
        in_specs=[
            pl.BlockSpec(memory_space=pltpu.SMEM),
            pl.BlockSpec(memory_space=pltpu.SMEM),
            pl.BlockSpec(memory_space=pltpu.VMEM),
            pl.BlockSpec(memory_space=pltpu.VMEM),
        ],
        out_specs=pl.BlockSpec(memory_space=pltpu.VMEM),
        scratch_shapes=scratch,
        compiler_params=pltpu.CompilerParams(vmem_limit_bytes=40 * 1024 * 1024),
        name="synthesis",
    )(own_orders, norm_logs(), geometry(), coefficients)


def relax_kernel(recv_ref, th_ref, tl_ref, rows_ref, pot_ref, mag_ref, dh_ref, dl_ref, turn_ref, plane_ref):
    for p in range(PAIRS_LOCAL):
        rest = recv_ref[pl.ds(16 + p // 2, LAT, stride=CHUNKS), :]
        for hx in range(4):
            chunk = p * 4 + hx
            main = recv_ref[pl.ds(chunk, LAT, stride=CHUNKS), :]
            offset = (p % 2) * 64 + hx * 16
            tail = pltpu.roll(rest, (128 - offset) % 128, 1) if offset else rest
            mh, ml = split2(main)
            eh, el = split2(tail)
            dh_ref[chunk * LAT:chunk * LAT + LAT, 0:128] = mh
            dl_ref[chunk * LAT:chunk * LAT + LAT, 0:128] = ml
            dh_ref[chunk * LAT:chunk * LAT + LAT, 128:256] = eh
            dl_ref[chunk * LAT:chunk * LAT + LAT, 128:256] = el
    dh, dl = dh_ref[...], dl_ref[...]
    th, tl = th_ref[...], tl_ref[...]
    turn_ref[0:COLS, :] = dot(th, dh) + dot(tl, dh) + dot(th, dl)
    turn_ref[COLS:, :] = jnp.zeros((384 - COLS, 256), jnp.float32)
    for j in range(3):
        plane_ref[j, 0:128, :] = turn_ref[128 * j:128 * j + 128, 0:128].T
        plane_ref[j, 128:256, :] = turn_ref[128 * j:128 * j + 128, 128:256].T
    planes = [
        jnp.concatenate([plane_ref[j, pl.ds(cr, EXT, stride=6), :] for j in range(3)], axis=1)
        for cr in range(6)
    ]
    field = [[planes[c * 2 + r] for r in range(2)] for c in range(3)]
    scale = jnp.concatenate([rows_ref[0]] * 3, axis=1)
    inside = jnp.concatenate([rows_ref[1]] * 3, axis=1) > 0.5

    def d_theta(a):
        return 0.5 * (pltpu.roll(a, EXT - 1, 0) - pltpu.roll(a, 1, 0))

    def d_phi(a):
        return (pltpu.roll(a, 383, 1) - pltpu.roll(a, 1, 1)) * scale

    def d_rad(pair):
        return [0.5 * pair[1], -0.5 * pair[0]]

    def curl(f):
        rad, colat, lon = f
        lon_r, colat_r = d_rad(lon), d_rad(colat)
        return [
            [d_theta(lon[r]) - d_phi(colat[r]) for r in range(2)],
            [d_phi(rad[r]) - lon_r[r] for r in range(2)],
            [colat_r[r] - d_theta(rad[r]) for r in range(2)],
        ]

    def cross(a, b):
        return [a[1] * b[2] - a[2] * b[1], a[2] * b[0] - a[0] * b[2], a[0] * b[1] - a[1] * b[0]]

    magnetic = None
    for _ in range(STEPS):
        magnetic = [[jnp.where(inside, b, 0.0) for b in pair] for pair in curl(field)]
        current = curl(magnetic)
        for r in range(2):
            b = [magnetic[c][r] for c in range(3)]
            j = [current[c][r] for c in range(3)]
            weight = 1.0 / (b[0] * b[0] + b[1] * b[1] + b[2] * b[2] + soft_floor)
            velocity = [f * weight for f in cross(j, b)]
            push = cross(velocity, b)
            for c in range(3):
                moved = field[c][r] + time_step * (push[c] - resist * j[c])
                field[c][r] = jnp.where(inside, moved, 0.0)

    def centre(a):
        a = pltpu.roll(pltpu.roll(a, EXT - HALO, 0), 384 - HALO, 1)
        return a[0:BAND, 0:SECTOR]

    for c in range(3):
        for r in range(2):
            pot_ref[c, r] = centre(field[c][r])
            mag_ref[c, r] = centre(magnetic[c][r])


def relax(received, table_high, table_low, rows):
    shape = jax.ShapeDtypeStruct((3, 2, BAND, SECTOR), jnp.float32)
    vmem = pl.BlockSpec(memory_space=pltpu.VMEM)
    return pl.pallas_call(
        relax_kernel,
        out_shape=(shape, shape),
        in_specs=[vmem] * 4,
        out_specs=(vmem, vmem),
        scratch_shapes=[
            pltpu.VMEM((1024, 256), jnp.bfloat16),
            pltpu.VMEM((1024, 256), jnp.bfloat16),
            pltpu.VMEM((384, 256), jnp.float32),
            pltpu.VMEM((3, 256, 128), jnp.float32),
        ],
        compiler_params=pltpu.CompilerParams(vmem_limit_bytes=40 * 1024 * 1024),
        name="relaxation",
    )(received, table_high, table_low, rows)


def per_device(coefficients, pair_orders):
    lat_pos = lax.axis_index("lat")
    lon_pos = lax.axis_index("lon")
    own_orders = lax.dynamic_slice_in_dim(pair_orders, lat_pos * PAIRS_LOCAL, PAIRS_LOCAL)
    send = synthesize(own_orders, coefficients).reshape(LAT, 1, CHUNKS * 128)
    received = lax.all_to_all(
        send, "lat", split_axis=0, concat_axis=0, tiled=True, axis_index_groups=[EXCHANGE]
    ).reshape(LAT * CHUNKS, 128)

    by_pair = pair_orders.reshape(LAT, PAIRS_LOCAL)
    by_pair = jnp.concatenate([by_pair[:HALF], by_pair[HALF:][::-1]], axis=0).T
    orders = jnp.stack([by_pair, ORDERS - 1 - by_pair], axis=1)
    orders = jnp.broadcast_to(orders[:, :, None, :], (PAIRS_LOCAL, 2, 2, LAT)).reshape(1, 1024)
    is_cos = (jnp.arange(1024, dtype=jnp.int32)[None, :] // LAT) % 2 == 0
    columns = lon_pos * SECTOR - HALO + jnp.arange(COLS, dtype=jnp.int32)[:, None]
    turns = (orders * columns + jnp.where(is_cos, NP // 4, 0)) & (NP - 1)
    table = jnp.sin(turns.astype(jnp.float32) * (2.0 * math.pi / NP))
    rounded = lax.reduce_precision(table, exponent_bits=8, mantissa_bits=7)
    table_high = rounded.astype(jnp.bfloat16)
    table_low = (table - rounded).astype(jnp.bfloat16)

    row_ids = lat_pos * BAND - HALO + jnp.arange(EXT, dtype=jnp.int32)
    theta = span_start + (row_ids.astype(jnp.float32) + 0.5) * (span_width / NT)
    scale = 1.0 / (2.0 * (3.0 * NT / NP) * jnp.sin(theta))
    inside = ((row_ids >= 0) & (row_ids < NT)).astype(jnp.float32)
    rows = jnp.broadcast_to(jnp.stack([scale, inside])[:, :, None], (2, EXT, 128))
    return relax(received, table_high, table_low, rows)


def solution(mesh):
    in_specs = (P("lat", None, None, None, None), P())
    out_specs = (P(None, None, "lat", "lon"), P(None, None, "lat", "lon"))
    return jax.shard_map(
        per_device, mesh=mesh, in_specs=in_specs, out_specs=out_specs, check_vma=False
    )
```

time: 1140 us -> 49 us (0.04)
  the two profiles are of different devices: /device:TPU:40 before, /device:TPU:16 now
where the time goes in v1:
time: 49 us; the launch traced here: 48.7 us
  waiting for transfers between devices  15.5 us (32%)
  starting transfers between devices  14.9 us (30%)
  Pallas kernels  9.61 us (20%)
  other arithmetic  4.35 us (9%)
  local copies, waits for them, and re-layouts  3.59 us (7%)
  between operations  0.74 us (2%)
    all_to_all x1, waiting for transfers between devices, per_device(): lax.all_to_all(send, 'lat', split_axis=0, concat_axis=0, tiled=True, axis...  15.5 us
    all_to_all x1, starting transfers between devices, per_device(): lax.all_to_all(send, 'lat', split_axis=0, concat_axis=0, tiled=True, axis...  14.9 us
    pallas_call x1, Pallas kernels, synthesize(): pl.pallas_call(synth_kernel, out_shape=jax.ShapeDtypeStruct((LAT * CHUNKS...  7.46 us
    convert_element_type x1, other arithmetic, per_device(): table_low = (table - rounded).astype(jnp.bfloat16)  4.11 us
    unnamed x8, local copies, waits for them, and re-layouts  2.3 us
    pallas_call x1, Pallas kernels, relax(): pl.pallas_call(relax_kernel, out_shape=(shape, shape), in_specs=[vmem] *...  2.15 us
  transfers between devices with their start and end apart: 1, of which 1 were waited for; matrix products, arithmetic and copies ran while one was open for 10% of the time, Pallas kernels for 0%

profile of v1, /device:TPU:16, one launch (start us, length us, event | category | flops | bytes accessed | tf_op | source)
XLA Modules:
  0.0 48.7 jit_solution(14922579046466024428)
XLA Ops:
  0.6 0.8 %dynamic_slice.3.order_ref = s32[4]{0:T(128)S(1)} dynamic-slice(s32[256]{0:T(256)} %param.5, s32[]{:T(128)S(6)} %select_n.34), dynamic_slice_sizes={4} | dynamic-slice | bytes 36 | tf_op jit(solution)/shard_map/dynamic_slice | solution.py:371
  1.4 0.0 copy-start
  1.4 0.9 %copy-done = f32[4,2,3,2,513]{4,3,2,1,0:T(2,128)S(1)} copy-done((f32[4,2,3,2,513]{4,3,2,1,0:T(2,128)S(1)}, f32[4,2,3,2,513]{4,3,2,1,0:T(2,128)}, u32[]{:S(2)}) %copy-start) | copy-done | bytes 98520
  2.3 0.0 copy-start.1
  2.3 0.7 %copy-done.1 = f32[4,8,128]{2,1,0:T(8,128)S(1)} copy-done((f32[4,8,128]{2,1,0:T(8,128)S(1)}, f32[4,8,128]{2,1,0:T(8,128)}, u32[]{:S(2)}) %copy-start.1) | copy-done | bytes 16408
  3.0 0.0 copy-start.2
  3.0 0.7 %copy-done.2 = f32[512]{0:T(512)S(1)} copy-done((f32[512]{0:T(512)S(1)}, f32[512]{0:T(512)}, u32[]{:S(2)}) %copy-start.2) | copy-done | bytes 2072
  3.7 7.5 %synthesis.1 = f32[1152,128]{1,0:T(8,128)} custom-call(s32[4]{0:T(128)S(1)} %dynamic_slice.3.order_ref, f32[512]{0:T(512)S(1)} %copy-done.2, f32[4,8,128]{2,1,0:T(8,128)S(1)} %copy-done.1, f32[4,2,3,2,513]{4,3,2,1,0:T(2,128)S(1)} %copy-done), custom_call_target="tpu_custom_call" | custom-call | tf_op jit(solution)/shard_map/synthesis/pallas_call | solution.py:259
  11.2 0.0 copy-start.3
  11.2 14.9 %all-to-all-start = ((f32[64,1,2304]{2,1,0:T(1,128)}), f32[64,1,2304]{2,1,0:T(1,128)S(1)}, u32[]{:S(2)}, u32[]{:S(2)}) async-start(f32[64,1,2304]{2,1,0:T(1,128)} %bitcast), calls=%async_computation | async-start | bytes 1179648 | tf_op jit(solution)/shard_map/all_to_all | solution.py:373
  26.1 0.0 copy-done.3
  26.1 0.1 slice.29
  26.2 0.1 copy.9
  26.3 0.1 slice.31
  26.4 0.1 copy.10
  26.5 0.1 fusion.8
  26.6 0.1 fusion.7
  26.7 0.1 mul.51
  26.8 0.1 multiply_divide_fusion
  26.9 4.1 %fusion = (bf16[272,1024]{1,0:T(8,128)(2,1)S(1)}, bf16[272,1024]{1,0:T(8,128)(2,1)S(1)}) fusion(s32[1024]{0:T(1024)S(1)} %fusion.6, s32[272]{0:T(512)S(1)} %iota_add_fusion, s32[1024]{0:T(1024)S(1)} %mul.51), kind=kLoop, calls=%fused_computation.2 | loop fusion | flops 2506752 | bytes 1123392 | tf_op jit(solution)/shard_map/convert_element_type | solution.py:387
  31.0 15.5 %all-to-all-done = f32[64,1,2304]{2,1,0:T(1,128)S(1)} async-done(((f32[64,1,2304]{2,1,0:T(1,128)}), f32[64,1,2304]{2,1,0:T(1,128)S(1)}, u32[]{:S(2)}, u32[]{:S(2)}) %all-to-all-start) | async-done | bytes 589856 | tf_op jit(solution)/shard_map/all_to_all | solution.py:373
  46.5 0.1 broadcast_in_dim.12.rows_ref
  46.6 2.2 %relaxation.1 = (f32[3,2,16,256]{3,2,1,0:T(8,128)}, f32[3,2,16,256]{3,2,1,0:T(8,128)}) custom-call(f32[1152,128]{1,0:T(8,128)S(1)} %bitcast.11, bf16[272,1024]{1,0:T(8,128)(2,1)S(1)} %get-tuple-element.3.th_ref, bf16[272,1024]{1,0:T(8,128)(2,1)S(1)} %get-tuple-element.2.tl_ref, f32[2,24,128]{2,1,0:T(8,128)S(1)} %broadcast_in_dim.12.rows_ref), custom_call_target="tpu_custom_call" | custom-call | tf_op jit(solution)/shard_map/relaxation/pallas_call | solution.py:352
  (9 shorter events, 0.1 us)
Async XLA Ops:
  1.4 0.9 %copy-start = (f32[4,2,3,2,513]{4,3,2,1,0:T(2,128)S(1)}, f32[4,2,3,2,513]{4,3,2,1,0:T(2,128)}, u32[]{:S(2)}) copy-start(f32[4,2,3,2,513]{4,3,2,1,0:T(2,128)} %coef_ref.1) | copy-start | bytes 295492
  2.3 0.7 %copy-start.1 = (f32[4,8,128]{2,1,0:T(8,128)S(1)}, f32[4,8,128]{2,1,0:T(8,128)}, u32[]{:S(2)}) copy-start(f32[4,8,128]{2,1,0:T(8,128)} %constant.77.clone.geom_ref) | copy-start | bytes 49156
  3.0 0.7 %copy-start.2 = (f32[512]{0:T(512)S(1)}, f32[512]{0:T(512)}, u32[]{:S(2)}) copy-start(f32[512]{0:T(512)} %constant.76.clone.log_ref) | copy-start | bytes 6148
  11.2 15.0 %copy-start.3 = (s32[256]{0:T(256)S(1)}, s32[256]{0:T(256)}, u32[]{:S(2)}) copy-start(s32[256]{0:T(256)} %param.5) | copy-start | bytes 3076
  11.2 35.3 %all-to-all-start = ((f32[64,1,2304]{2,1,0:T(1,128)}), f32[64,1,2304]{2,1,0:T(1,128)S(1)}, u32[]{:S(2)}, u32[]{:S(2)}) async-start(f32[64,1,2304]{2,1,0:T(1,128)} %bitcast), calls=%async_computation | async-start | bytes 1179648 | tf_op jit(solution)/shard_map/all_to_all | solution.py:373

commit v2 on v1

v2 whole, which is shorter than its diff:
```python
import math

import jax
import jax.numpy as jnp
import numpy as np
from jax import lax
from jax.experimental import pallas as pl
from jax.experimental.pallas import tpu as pltpu
from jax.sharding import PartitionSpec as P

ORDERS = 512
NT = 1024
NP = 2048
STEPS = 2
LAT = 64
LON = 8
BAND = NT // LAT
SECTOR = NP // LON
HALO = 4
EXT = BAND + 2 * HALO
PAIRS_LOCAL = 4
HALF = LAT // 2
CHUNKS = 9
COLS = SECTOR + 16

soft_floor = 1.0
resist = 0.2
time_step = 0.3
rescale_at = 1.0e10
block_steps = 16
span_start = math.pi / 6.0
span_width = 2.0 * math.pi / 3.0

EXCHANGE = list(range(HALF)) + [LAT - 1 - u for u in range(HALF)]


def own_rows(core):
    first = [2 * core, 2 * core + 1, 4 + 2 * core, 5 + 2 * core]
    return first + [BAND - 1 - r for r in reversed(first)]


def geometry():
    own = np.array([own_rows(0), own_rows(1)])
    rows = BAND * np.arange(HALF)[None, None, :] + own[:, :, None]
    theta = span_start + (rows + 0.5) * (span_width / NT)
    cosine = np.tile(np.cos(theta), (1, 1, PAIRS_LOCAL))
    log_sin = np.tile(np.log(np.sin(theta)), (1, 1, PAIRS_LOCAL))
    return np.stack([cosine, log_sin], axis=1).astype(np.float32)


def norm_logs():
    k = np.arange(1, ORDERS, dtype=np.float64)
    logs = np.concatenate([[0.0], np.cumsum(0.5 * np.log((2 * k + 1) / (2 * k)))])
    return (logs - 0.5 * np.log(4 * np.pi)).astype(np.float32)


def split2(value):
    high = value.astype(jnp.bfloat16)
    low = (value - high.astype(jnp.float32)).astype(jnp.bfloat16)
    return high, low


def dot(a, b):
    return jnp.dot(a, b, preferred_element_type=jnp.float32)


def synth_kernel(
    order_hbm, log_hbm, geom_hbm, coef_hbm, out_ref,
    order_ref, log_ref, geom_ref, coef_ref, fac_ref, back_ref, leg_ref, coefs_ref, wh_ref, wl_ref, stack_ref,
    sems,
):
    lat_pos = lax.axis_index("lat")
    core = lax.axis_index("lon") % 2
    copies = [
        pltpu.make_async_copy(order_hbm, order_ref, sems.at[0]),
        pltpu.make_async_copy(log_hbm, log_ref, sems.at[1]),
        pltpu.make_async_copy(geom_hbm.at[core], geom_ref, sems.at[2]),
        pltpu.make_async_copy(coef_hbm, coef_ref, sems.at[3]),
    ]
    for copy in copies:
        copy.start()
    coefs_ref[...] = jnp.zeros_like(coefs_ref)
    lane = lax.broadcasted_iota(jnp.int32, (8, 128), 1)
    pair_of_lane = lane // HALF

    def per_pair(values):
        result = jnp.full((8, 128), values[0], values[0].dtype)
        for p in range(1, PAIRS_LOCAL):
            result = jnp.where(pair_of_lane == p, values[p], result)
        return result

    copies[0].wait()
    lows = [order_ref[lat_pos * PAIRS_LOCAL + p] for p in range(PAIRS_LOCAL)]
    low = per_pair([o.astype(jnp.float32) for o in lows])
    high = (ORDERS - 1.0) - low
    switch = ORDERS - low

    for c in range(65):
        step = lax.broadcasted_iota(jnp.int32, (8, 128), 0).astype(jnp.float32) + float(8 * c)
        if c < 32:
            order, degree = low, low + step
        else:
            low_side = step < switch
            order = jnp.where(low_side, low, high)
            degree = jnp.where(low_side, low + step, step - 1.0)
        prior = degree - 1.0
        order2 = order * order
        degree2 = degree * degree
        prior2 = prior * prior
        factor = jnp.sqrt(jnp.maximum(4.0 * degree2 - 1.0, 1.0) / jnp.maximum(degree2 - order2, 1.0))
        back = jnp.sqrt(jnp.maximum(prior2 - order2, 0.0) / jnp.maximum(4.0 * prior2 - 1.0, 1.0))
        fac_ref[8 * c:8 * c + 8, :] = factor
        back_ref[8 * c:8 * c + 8, :] = jnp.where(prior > order, factor * back, 0.0)

    copies[1].wait()
    copies[2].wait()
    cosine = geom_ref[0]
    log_sin = geom_ref[1]
    norm_low = per_pair([log_ref[o] for o in lows])
    norm_high = per_pair([log_ref[ORDERS - 1 - o] for o in lows])
    seed_low = norm_low + low * log_sin
    seed_high = norm_high + high * log_sin
    start_scale = jnp.exp(seed_high)
    log_big = math.log(rescale_at)

    def run(base, count, state, restart, first):
        previous, current, scaling, scale = state
        for k in range(count):
            s = base + k
            fac = fac_ref[pl.ds(s, 1), :]
            back = back_ref[pl.ds(s, 1), :]
            if first and k == 0:
                value = jnp.ones((8, 128), jnp.float32)
            else:
                value = (fac * cosine) * current - back * previous
            if restart:
                starting = switch == (s.astype(jnp.float32) if not isinstance(s, int) else float(s))
                value = jnp.where(starting, 1.0, value)
                scaling = jnp.where(starting, seed_high, scaling)
                scale = jnp.where(starting, start_scale, scale)
            previous, current = current, value
            at = s * 8 if isinstance(s, int) else pl.multiple_of(s * 8, 8)
            leg_ref[pl.ds(at, 8), :] = value * scale
        big = jnp.abs(current) > rescale_at
        shrink = jnp.where(big, 1.0 / rescale_at, 1.0)
        scaling = scaling + jnp.where(big, log_big, 0.0)
        return previous * shrink, current * shrink, scaling, jnp.exp(scaling)

    zero = jnp.zeros((8, 128), jnp.float32)
    state = run(0, block_steps, (zero, zero, seed_low, jnp.exp(seed_low)), False, True)
    state = lax.fori_loop(
        1, 16, lambda b, st: run(b * block_steps, block_steps, st, False, False), state
    )
    state = lax.fori_loop(
        16, 32, lambda b, st: run(b * block_steps, block_steps, st, True, False), state
    )
    run(512, 1, state, True, False)

    copies[3].wait()
    for p in range(PAIRS_LOCAL):
        for x in range(2):
            for c in range(3):
                row = (p * 2 + x) * 8 + c * 2
                coefs_ref[row:row + 2, 0:513] = coef_ref[p, x, c]
    slot = lax.broadcasted_iota(jnp.int32, (8, 512), 1)
    for p in range(PAIRS_LOCAL):
        is_low = slot < ORDERS - lows[p]
        low_sign = 1.0 - 2.0 * (slot % 2).astype(jnp.float32)
        high_sign = 1.0 - 2.0 * ((slot + lows[p]) % 2).astype(jnp.float32)
        for x in range(2):
            row = (p * 2 + x) * 8
            both = coefs_ref[row:row + 8, 0:512]
            parts = [jnp.where(is_low, both, 0.0), jnp.where(is_low, 0.0, both)]
            for side in range(2):
                for h in range(2):
                    w = parts[h] if side == 0 else parts[h] * (low_sign if h == 0 else high_sign)
                    at = (((side * PAIRS_LOCAL + p) * 2 + h) * 2 + x) * 8
                    wh, wl = split2(w)
                    wh_ref[at:at + 8, :] = wh.astype(jnp.float32)
                    wl_ref[at:at + 8, :] = wl.astype(jnp.float32)

    tail_sign = per_pair([1.0 - 2.0 * (o % 2).astype(jnp.float32) for o in lows])
    tails = []
    for x in range(2):
        tail = jnp.zeros((8, 128), jnp.float32)
        for p in range(PAIRS_LOCAL):
            row = (p * 2 + x) * 8
            column = jnp.broadcast_to(coefs_ref[row:row + 8, 512:513], (8, 128))
            tail = jnp.where(pair_of_lane == p, column, tail)
        tails.append(tail)
    wh = wh_ref[...].astype(jnp.bfloat16)
    wl = wl_ref[...].astype(jnp.bfloat16)
    for t0 in range(0, 8, 2):
        values = jnp.concatenate(
            [leg_ref[pl.ds(t0 + d, 512, stride=8), :] for d in range(2)], axis=1
        )
        vh, vl = split2(values)
        summed = dot(wh, vh) + dot(wl, vh) + dot(wh, vl)
        for d in range(2):
            t = t0 + d
            last = leg_ref[pl.ds(512 * 8 + t, 1), :]
            part = summed[:, 128 * d:128 * d + 128]
            for side in range(2):
                for h in range(2):
                    for x in range(2):
                        picked = None
                        for p in range(PAIRS_LOCAL):
                            at = (((side * PAIRS_LOCAL + p) * 2 + h) * 2 + x) * 8
                            block = part[at:at + 8, :]
                            picked = block if p == 0 else jnp.where(pair_of_lane == p, block, picked)
                        if h == 1:
                            term = tails[x] * last
                            picked = picked + (term if side == 0 else term * tail_sign)
                        q = 2 + (t if side == 0 else 7 - t)
                        stack_ref[(side * 2 + h) * 2 + x, 6 * q:6 * q + 6, :] = picked[0:6]

    unit = lax.broadcasted_iota(jnp.int32, (12, 128), 1) % HALF
    for h in range(2):
        for x in range(2):
            north, south = h * 2 + x, 4 + h * 2 + x
            n_first, n_last = stack_ref[north, 12:24, :], stack_ref[north, 48:60, :]
            s_first, s_last = stack_ref[south, 12:24, :], stack_ref[south, 48:60, :]
            stack_ref[north, 0:12, :] = jnp.where(unit == 0, 0.0, pltpu.roll(n_last, 1, 1))
            stack_ref[north, 60:72, :] = jnp.where(unit == HALF - 1, s_first, pltpu.roll(n_first, 127, 1))
            stack_ref[south, 0:12, :] = jnp.where(unit == HALF - 1, n_last, pltpu.roll(s_last, 127, 1))
            stack_ref[south, 60:72, :] = jnp.where(unit == 0, 0.0, pltpu.roll(s_first, 1, 1))

    group = lax.broadcasted_iota(jnp.int32, (HALF, 128), 1) // HALF
    for side in range(2):
        for h in range(2):
            which = (side * 2 + h) * 2
            turned = jnp.concatenate([stack_ref[which, 0:64, :], stack_ref[which + 1, 0:64, :]], axis=0).T
            for p in range(PAIRS_LOCAL):
                out_ref[pl.ds(side * HALF * CHUNKS + p * 2 + h, HALF, stride=CHUNKS), :] = turned[
                    HALF * p:HALF * p + HALF, :
                ]
        rest = jnp.concatenate([stack_ref[side * 4 + k, 64:72, :] for k in range(4)] * PAIRS_LOCAL, axis=0).T
        picked = rest[0:HALF, :]
        for p in range(1, PAIRS_LOCAL):
            picked = jnp.where(group == p, rest[HALF * p:HALF * p + HALF, :], picked)
        out_ref[pl.ds(side * HALF * CHUNKS + 8, HALF, stride=CHUNKS), :] = picked


def synthesize(pair_orders, coefficients):
    hbm = pl.BlockSpec(memory_space=pltpu.HBM)
    scratch = [
        pltpu.SMEM((256,), jnp.int32),
        pltpu.SMEM((512,), jnp.float32),
        pltpu.VMEM((2, 8, 128), jnp.float32),
        pltpu.VMEM((4, 2, 3, 2, 513), jnp.float32),
        pltpu.VMEM((520, 128), jnp.float32),
        pltpu.VMEM((520, 128), jnp.float32),
        pltpu.VMEM((520 * 8, 128), jnp.float32),
        pltpu.VMEM((64, 640), jnp.float32),
        pltpu.VMEM((256, 512), jnp.float32),
        pltpu.VMEM((256, 512), jnp.float32),
        pltpu.VMEM((8, 72, 128), jnp.float32),
        pltpu.SemaphoreType.DMA((4,)),
    ]
    return pl.pallas_call(
        synth_kernel,
        out_shape=jax.ShapeDtypeStruct((LAT * CHUNKS, 128), jnp.float32),
        in_specs=[hbm] * 4,
        out_specs=pl.BlockSpec(memory_space=pltpu.VMEM),
        scratch_shapes=scratch,
        compiler_params=pltpu.CompilerParams(vmem_limit_bytes=60 * 1024 * 1024),
        name="synthesis",
    )(pair_orders, norm_logs(), geometry(), coefficients)


def relax_kernel(recv_ref, th_ref, tl_ref, rows_ref, pot_ref, mag_ref, dh_ref, dl_ref, turn_ref, plane_ref):
    lane = lax.broadcasted_iota(jnp.int32, (LAT, 128), 1)
    for half in range(2):
        start = half * LAT * CHUNKS
        at = half * 128
        rest = recv_ref[pl.ds(start + 8, LAT, stride=CHUNKS), :]
        for both in range(8):
            main = recv_ref[pl.ds(start + both, LAT, stride=CHUNKS), :]
            for x in range(2):
                ox = both * 2 + x
                head = pltpu.roll(main, 64, 1) if x else main
                shift = (64 - 8 * ox) % 128
                tail = pltpu.roll(rest, shift, 1) if shift else rest
                high, low = split2(jnp.where(lane < 64, head, tail))
                dh_ref[ox * LAT:ox * LAT + LAT, at:at + 128] = high
                dl_ref[ox * LAT:ox * LAT + LAT, at:at + 128] = low
    dh, dl = dh_ref[...], dl_ref[...]
    th, tl = th_ref[...], tl_ref[...]
    turn_ref[0:COLS, :] = dot(th, dh) + dot(tl, dh) + dot(th, dl)
    turn_ref[COLS:, :] = jnp.zeros((384 - COLS, 256), jnp.float32)
    for j in range(3):
        for half in range(2):
            turned = turn_ref[128 * j:128 * j + 128, 128 * half:128 * half + 128].T
            starts = [2 - 2 * half] + [HALO + r for r in own_rows(half)[::2]] + [20 + 2 * half]
            for k, e in enumerate(starts):
                plane_ref[j, 6 * e:6 * e + 12, :] = turned[12 * k:12 * k + 12, :]
    planes = [
        jnp.concatenate([plane_ref[j, pl.ds(cr, EXT, stride=6), :] for j in range(3)], axis=1)
        for cr in range(6)
    ]
    field = [[planes[c * 2 + r] for r in range(2)] for c in range(3)]
    scale = jnp.concatenate([rows_ref[0]] * 3, axis=1)
    inside = jnp.concatenate([rows_ref[1]] * 3, axis=1) > 0.5

    def d_theta(a):
        return 0.5 * (pltpu.roll(a, EXT - 1, 0) - pltpu.roll(a, 1, 0))

    def d_phi(a):
        return (pltpu.roll(a, 383, 1) - pltpu.roll(a, 1, 1)) * scale

    def d_rad(pair):
        return [0.5 * pair[1], -0.5 * pair[0]]

    def curl(f):
        rad, colat, lon = f
        lon_r, colat_r = d_rad(lon), d_rad(colat)
        return [
            [d_theta(lon[r]) - d_phi(colat[r]) for r in range(2)],
            [d_phi(rad[r]) - lon_r[r] for r in range(2)],
            [colat_r[r] - d_theta(rad[r]) for r in range(2)],
        ]

    def cross(a, b):
        return [a[1] * b[2] - a[2] * b[1], a[2] * b[0] - a[0] * b[2], a[0] * b[1] - a[1] * b[0]]

    magnetic = None
    for _ in range(STEPS):
        magnetic = [[jnp.where(inside, b, 0.0) for b in pair] for pair in curl(field)]
        current = curl(magnetic)
        for r in range(2):
            b = [magnetic[c][r] for c in range(3)]
            j = [current[c][r] for c in range(3)]
            weight = 1.0 / (b[0] * b[0] + b[1] * b[1] + b[2] * b[2] + soft_floor)
            velocity = [f * weight for f in cross(j, b)]
            push = cross(velocity, b)
            for c in range(3):
                moved = field[c][r] + time_step * (push[c] - resist * j[c])
                field[c][r] = jnp.where(inside, moved, 0.0)

    def centre(a):
        a = pltpu.roll(pltpu.roll(a, EXT - HALO, 0), 384 - HALO, 1)
        return a[0:BAND, 0:SECTOR]

    for c in range(3):
        for r in range(2):
            pot_ref[c, r] = centre(field[c][r])
            mag_ref[c, r] = centre(magnetic[c][r])


def relax(received, table_high, table_low, rows):
    shape = jax.ShapeDtypeStruct((3, 2, BAND, SECTOR), jnp.float32)
    vmem = pl.BlockSpec(memory_space=pltpu.VMEM)
    return pl.pallas_call(
        relax_kernel,
        out_shape=(shape, shape),
        in_specs=[vmem] * 4,
        out_specs=(vmem, vmem),
        scratch_shapes=[
            pltpu.VMEM((1024, 256), jnp.bfloat16),
            pltpu.VMEM((1024, 256), jnp.bfloat16),
            pltpu.VMEM((384, 256), jnp.float32),
            pltpu.VMEM((3, 144, 128), jnp.float32),
        ],
        compiler_params=pltpu.CompilerParams(vmem_limit_bytes=40 * 1024 * 1024),
        name="relaxation",
    )(received, table_high, table_low, rows)


def per_device(coefficients, pair_orders):
    lat_pos = lax.axis_index("lat")
    lon_pos = lax.axis_index("lon")
    send = synthesize(pair_orders, coefficients).reshape(LAT, 1, CHUNKS * 128)
    half = lax.all_to_all(
        send, "lat", split_axis=0, concat_axis=0, tiled=True, axis_index_groups=[EXCHANGE]
    ).reshape(LAT * CHUNKS, 128)
    cores = [[2 * i, 2 * i + 1] for i in range(LON // 2)]
    received = lax.all_gather(half, "lon", axis=0, tiled=True, axis_index_groups=cores)

    by_pair = pair_orders.reshape(LAT, PAIRS_LOCAL)
    by_pair = jnp.concatenate([by_pair[:HALF], by_pair[HALF:][::-1]], axis=0).T
    orders = jnp.stack([by_pair, ORDERS - 1 - by_pair], axis=1)
    orders = jnp.broadcast_to(orders[:, :, None, :], (PAIRS_LOCAL, 2, 2, LAT)).reshape(1, 1024)
    is_cos = (jnp.arange(1024, dtype=jnp.int32)[None, :] // LAT) % 2 == 0
    columns = lon_pos * SECTOR - HALO + jnp.arange(COLS, dtype=jnp.int32)[:, None]
    turns = (orders * columns + jnp.where(is_cos, NP // 4, 0)) & (NP - 1)
    table = jnp.sin(turns.astype(jnp.float32) * (2.0 * math.pi / NP))
    rounded = lax.reduce_precision(table, exponent_bits=8, mantissa_bits=7)
    table_high = rounded.astype(jnp.bfloat16)
    table_low = (table - rounded).astype(jnp.bfloat16)

    row_ids = lat_pos * BAND - HALO + jnp.arange(EXT, dtype=jnp.int32)
    theta = span_start + (row_ids.astype(jnp.float32) + 0.5) * (span_width / NT)
    scale = 1.0 / (2.0 * (3.0 * NT / NP) * jnp.sin(theta))
    inside = ((row_ids >= 0) & (row_ids < NT)).astype(jnp.float32)
    rows = jnp.broadcast_to(jnp.stack([scale, inside])[:, :, None], (2, EXT, 128))
    return relax(received, table_high, table_low, rows)


def solution(mesh):
    in_specs = (P("lat", None, None, None, None), P())
    out_specs = (P(None, None, "lat", "lon"), P(None, None, "lat", "lon"))
    return jax.shard_map(
        per_device, mesh=mesh, in_specs=in_specs, out_specs=out_specs, check_vma=False
    )
```

time: 49 us -> 40.7 us (0.83)
  the two profiles are of different devices: /device:TPU:16 before, /device:TPU:1 now
where the time goes in v2:
time: 40.7 us; the launch traced here: 40.6 us
  starting transfers between devices  15.4 us (38%)
  waiting for transfers between devices  7.94 us (20%)
  Pallas kernels  7.54 us (19%)
  other arithmetic  4.34 us (11%)
  blocking collectives  4.11 us (10%)
  between operations  0.74 us (2%)
  local copies, waits for them, and re-layouts  0.53 us (1%)
    all_to_all x1, starting transfers between devices, per_device(): lax.all_to_all(send, 'lat', split_axis=0, concat_axis=0, tiled=True, axis...  15.4 us
    all_to_all x1, waiting for transfers between devices, per_device(): lax.all_to_all(send, 'lat', split_axis=0, concat_axis=0, tiled=True, axis...  7.94 us
    pallas_call x1, Pallas kernels, synthesize(): pl.pallas_call(synth_kernel, out_shape=jax.ShapeDtypeStruct((LAT * CHUNKS...  5.04 us
    all_gather x1, blocking collectives, per_device(): lax.all_gather(half, 'lon', axis=0, tiled=True, axis_index_groups=cores)  4.11 us
    convert_element_type x1, other arithmetic, per_device(): table_low = (table - rounded).astype(jnp.bfloat16)  4.11 us
    pallas_call x1, Pallas kernels, relax(): pl.pallas_call(relax_kernel, out_shape=(shape, shape), in_specs=[vmem] *...  2.5 us
  transfers between devices with their start and end apart: 1, of which 1 were waited for; matrix products, arithmetic and copies ran while one was open for 12% of the time, Pallas kernels for 0%

profile of v2, /device:TPU:1, one launch (start us, length us, event | category | flops | bytes accessed | tf_op | source)
XLA Modules:
  0.0 40.6 jit_solution(4423830692099528797)
XLA Ops:
  0.6 0.0 copy-start
  0.6 5.0 %synthesis.1 = f32[576,128]{1,0:T(8,128)} custom-call(s32[256]{0:T(256)} %order_hbm.1, f32[512]{0:T(512)} %constant.75.clone.log_hbm, f32[2,2,8,128]{3,2,1,0:T(8,128)} %constant.76.clone.geom_hbm, f32[4,2,3,2,513]{4,3,2,1,0:T(2,128)} %coef_hbm.1), custom_call_target="tpu_custom_call" | custom-call | tf_op jit(solution)/shard_map/synthesis/pallas_call | solution.py:260
  5.7 15.4 %all-to-all-start = ((f32[64,1,1152]{2,1,0:T(1,128)}), f32[64,1,1152]{2,1,0:T(1,128)S(1)}, u32[]{:S(2)}, u32[]{:S(2)}) async-start(f32[64,1,1152]{2,1,0:T(1,128)} %bitcast.12), calls=%async_computation | async-start | bytes 589824 | tf_op jit(solution)/shard_map/all_to_all | solution.py:373
  21.1 0.0 copy-done
  21.1 0.1 slice.29
  21.2 0.1 copy.9
  21.3 0.1 slice.31
  21.4 0.1 copy.10
  21.5 0.1 fusion.8
  21.6 0.1 fusion.7
  21.7 0.1 mul.47
  21.8 4.1 %fusion = (bf16[272,1024]{1,0:T(8,128)(2,1)S(1)}, bf16[272,1024]{1,0:T(8,128)(2,1)S(1)}) fusion(s32[1024]{0:T(1024)S(1)} %fusion.6, s32[272]{0:T(512)S(1)} %iota_add_fusion, s32[1024]{0:T(1024)S(1)} %mul.47), kind=kLoop, calls=%fused_computation.2 | loop fusion | flops 2506752 | bytes 1123392 | tf_op jit(solution)/shard_map/convert_element_type | solution.py:389
  25.9 7.9 %all-to-all-done = f32[64,1,1152]{2,1,0:T(1,128)S(1)} async-done(((f32[64,1,1152]{2,1,0:T(1,128)}), f32[64,1,1152]{2,1,0:T(1,128)S(1)}, u32[]{:S(2)}, u32[]{:S(2)}) %all-to-all-start) | async-done | bytes 294944 | tf_op jit(solution)/shard_map/all_to_all | solution.py:373
  33.9 4.1 %all_gather.3.recv_ref = f32[1152,128]{1,0:T(8,128)S(1)} all-gather(f32[576,128]{1,0:T(8,128)S(1)} %bitcast.11), channel_id=1, replica_groups={{0,1},{2,3},{4,5},{6,7},{8,9},{10,11},{12,13},{14,15},{16,17},{18,19},{..., dimensions={0}, use_global_device_ids=true | all-gather | bytes 884736 | tf_op jit(solution)/shard_map/all_gather | solution.py:377
  38.0 0.1 broadcast_in_dim.12.rows_ref
  38.1 2.5 %relaxation.1 = (f32[3,2,16,256]{3,2,1,0:T(8,128)}, f32[3,2,16,256]{3,2,1,0:T(8,128)}) custom-call(f32[1152,128]{1,0:T(8,128)S(1)} %all_gather.3.recv_ref, bf16[272,1024]{1,0:T(8,128)(2,1)S(1)} %get-tuple-element.3.th_ref, bf16[272,1024]{1,0:T(8,128)(2,1)S(1)} %get-tuple-element.2.tl_ref, f32[2,24,128]{2,1,0:T(8,128)S(1)} %broadcast_in_dim.12.rows_ref), custom_call_target="tpu_custom_call" | custom-call | tf_op jit(solution)/shard_map/relaxation/pallas_call | solution.py:353
  (10 shorter events, 0.1 us)
Async XLA Ops:
  0.6 20.5 %copy-start = (s32[256]{0:T(256)S(1)}, s32[256]{0:T(256)}, u32[]{:S(2)}) copy-start(s32[256]{0:T(256)} %order_hbm.1) | copy-start | bytes 3076
  5.7 28.2 %all-to-all-start = ((f32[64,1,1152]{2,1,0:T(1,128)}), f32[64,1,1152]{2,1,0:T(1,128)S(1)}, u32[]{:S(2)}, u32[]{:S(2)}) async-start(f32[64,1,1152]{2,1,0:T(1,128)} %bitcast.12), calls=%async_computation | async-start | bytes 589824 | tf_op jit(solution)/shard_map/all_to_all | solution.py:373

commit v3 on v2

--- a/solution.py
+++ b/solution.py
@@ -31,7 +31,10 @@
 span_start = math.pi / 6.0
 span_width = 2.0 * math.pi / 3.0
 
-EXCHANGE = list(range(HALF)) + [LAT - 1 - u for u in range(HALF)]
+LAT_X, LAT_Z = 4, 8
+EXCHANGE = [
+    y * HALF + x * LAT_Z + z for y in range(2) for z in reversed(range(LAT_Z)) for x in range(LAT_X)
+]
 
 
 def own_rows(core):
@@ -226,15 +229,26 @@
             stack_ref[south, 60:72, :] = jnp.where(unit == 0, 0.0, pltpu.roll(s_first, 1, 1))
 
     group = lax.broadcasted_iota(jnp.int32, (HALF, 128), 1) // HALF
+    wide = lax.broadcasted_iota(jnp.int32, (128, 128), 1)
+    x, z = wide % LAT_X, (wide // LAT_X) % LAT_Z
+    base = wide // HALF * HALF
+    source = [base + x * LAT_Z + (LAT_Z - 1 - z), base + (LAT_X - 1 - x) * LAT_Z + z]
+
+    def by_member(value, side):
+        return jnp.take_along_axis(value, source[side], axis=1)
+
     for side in range(2):
         for h in range(2):
             which = (side * 2 + h) * 2
-            turned = jnp.concatenate([stack_ref[which, 0:64, :], stack_ref[which + 1, 0:64, :]], axis=0).T
+            turned = by_member(
+                jnp.concatenate([stack_ref[which, 0:64, :], stack_ref[which + 1, 0:64, :]], axis=0), side
+            ).T
             for p in range(PAIRS_LOCAL):
                 out_ref[pl.ds(side * HALF * CHUNKS + p * 2 + h, HALF, stride=CHUNKS), :] = turned[
                     HALF * p:HALF * p + HALF, :
                 ]
-        rest = jnp.concatenate([stack_ref[side * 4 + k, 64:72, :] for k in range(4)] * PAIRS_LOCAL, axis=0).T
+        rest = jnp.concatenate([stack_ref[side * 4 + k, 64:72, :] for k in range(4)] * PAIRS_LOCAL, axis=0)
+        rest = by_member(rest, side).T
         picked = rest[0:HALF, :]
         for p in range(1, PAIRS_LOCAL):
             picked = jnp.where(group == p, rest[HALF * p:HALF * p + HALF, :], picked)
@@ -377,7 +391,8 @@
     received = lax.all_gather(half, "lon", axis=0, tiled=True, axis_index_groups=cores)
 
     by_pair = pair_orders.reshape(LAT, PAIRS_LOCAL)
-    by_pair = jnp.concatenate([by_pair[:HALF], by_pair[HALF:][::-1]], axis=0).T
+    by_pair = by_pair.reshape(2, LAT_X, LAT_Z, PAIRS_LOCAL)[:, :, ::-1].transpose(3, 0, 2, 1)
+    by_pair = by_pair.reshape(PAIRS_LOCAL, LAT)
     orders = jnp.stack([by_pair, ORDERS - 1 - by_pair], axis=1)
     orders = jnp.broadcast_to(orders[:, :, None, :], (PAIRS_LOCAL, 2, 2, LAT)).reshape(1, 1024)
     is_cos = (jnp.arange(1024, dtype=jnp.int32)[None, :] // LAT) % 2 == 0

time: 40.7 us -> 37.5 us (0.921)
  waiting for transfers between devices: 7.94 us -> 4.08 us
  blocking collectives: 4.11 us -> 4.78 us
    all_to_all x1, waiting for transfers between devices: 7.94 us -> 4.08 us  [per_device(): lax.all_to_all(send, 'lat', split_axis=0, concat_axis=0, tiled=True, axis...]
    all_gather x1, blocking collectives: 4.11 us -> 4.78 us  [per_device(): lax.all_gather(half, 'lon', axis=0, tiled=True, axis_index_groups=cores)]
  transfers between devices with their start and end apart: 1 -> 1, of which waited for: 1 -> 1; matrix products, arithmetic and copies ran while one was open for 12% -> 13% of each run, Pallas kernels for 0% -> 0%
where the time goes in v3:
time: 37.5 us; the launch traced here: 37.3 us
  starting transfers between devices  15.3 us (41%)
  Pallas kernels  7.65 us (20%)
  blocking collectives  4.78 us (13%)
  other arithmetic  4.19 us (11%)
  waiting for transfers between devices  4.08 us (11%)
  between operations  0.74 us (2%)
  local copies, waits for them, and re-layouts  0.57 us (2%)
    all_to_all x1, starting transfers between devices, per_device(): lax.all_to_all(send, 'lat', split_axis=0, concat_axis=0, tiled=True, axis...  15.3 us
    pallas_call x1, Pallas kernels, synthesize(): pl.pallas_call(synth_kernel, out_shape=jax.ShapeDtypeStruct((LAT * CHUNKS...  5.15 us
    all_gather x1, blocking collectives, per_device(): lax.all_gather(half, 'lon', axis=0, tiled=True, axis_index_groups=cores)  4.78 us
    convert_element_type x1, other arithmetic, per_device(): table_low = (table - rounded).astype(jnp.bfloat16)  4.11 us
    all_to_all x1, waiting for transfers between devices, per_device(): lax.all_to_all(send, 'lat', split_axis=0, concat_axis=0, tiled=True, axis...  4.08 us
    pallas_call x1, Pallas kernels, relax(): pl.pallas_call(relax_kernel, out_shape=(shape, shape), in_specs=[vmem] *...  2.5 us
  transfers between devices with their start and end apart: 1, of which 1 were waited for; matrix products, arithmetic and copies ran while one was open for 13% of the time, Pallas kernels for 0%

profile of v3, /device:TPU:1, one launch (start us, length us, event | category | flops | bytes accessed | tf_op | source)
XLA Modules:
  0.0 37.3 jit_solution(396691381543485027)
XLA Ops:
  0.6 0.0 copy-start
  0.6 5.1 %synthesis.1 = f32[576,128]{1,0:T(8,128)} custom-call(s32[256]{0:T(256)} %order_hbm.1, f32[512]{0:T(512)} %constant.75.clone.log_hbm, f32[2,2,8,128]{3,2,1,0:T(8,128)} %constant.76.clone.geom_hbm, f32[4,2,3,2,513]{4,3,2,1,0:T(2,128)} %coef_hbm.1), custom_call_target="tpu_custom_call" | custom-call | tf_op jit(solution)/shard_map/synthesis/pallas_call | solution.py:274
  5.8 15.3 %all-to-all-start = ((f32[64,1,1152]{2,1,0:T(1,128)}), f32[64,1,1152]{2,1,0:T(1,128)S(1)}, u32[]{:S(2)}, u32[]{:S(2)}) async-start(f32[64,1,1152]{2,1,0:T(1,128)} %bitcast.6), calls=%async_computation | async-start | bytes 589824 | tf_op jit(solution)/shard_map/all_to_all | solution.py:387
  21.1 0.0 copy-done
  21.1 0.1 reshape_reshape.3
  21.3 0.2 copy.9
  21.5 0.1 stack_reshape.3
  21.6 0.1 mul.47
  21.7 4.1 %fusion = (bf16[272,1024]{1,0:T(8,128)(2,1)S(1)}, bf16[272,1024]{1,0:T(8,128)(2,1)S(1)}) fusion(s32[1024]{0:T(1024)S(1)} %fusion.6, s32[272]{0:T(512)S(1)} %iota_add_fusion, s32[1024]{0:T(1024)S(1)} %mul.47), kind=kLoop, calls=%fused_computation.2 | loop fusion | flops 2506752 | bytes 1123392 | tf_op jit(solution)/shard_map/convert_element_type | solution.py:404
  25.8 4.1 %all-to-all-done = f32[64,1,1152]{2,1,0:T(1,128)S(1)} async-done(((f32[64,1,1152]{2,1,0:T(1,128)}), f32[64,1,1152]{2,1,0:T(1,128)S(1)}, u32[]{:S(2)}, u32[]{:S(2)}) %all-to-all-start) | async-done | bytes 294944 | tf_op jit(solution)/shard_map/all_to_all | solution.py:387
  29.9 4.8 %all_gather.3.recv_ref = f32[1152,128]{1,0:T(8,128)S(1)} all-gather(f32[576,128]{1,0:T(8,128)S(1)} %bitcast.5), channel_id=1, replica_groups={{0,1},{2,3},{4,5},{6,7},{8,9},{10,11},{12,13},{14,15},{16,17},{18,19},{..., dimensions={0}, use_global_device_ids=true | all-gather | bytes 884736 | tf_op jit(solution)/shard_map/all_gather | solution.py:391
  34.7 0.1 broadcast_in_dim.12.rows_ref
  34.8 2.5 %relaxation.1 = (f32[3,2,16,256]{3,2,1,0:T(8,128)}, f32[3,2,16,256]{3,2,1,0:T(8,128)}) custom-call(f32[1152,128]{1,0:T(8,128)S(1)} %all_gather.3.recv_ref, bf16[272,1024]{1,0:T(8,128)(2,1)S(1)} %get-tuple-element.3.th_ref, bf16[272,1024]{1,0:T(8,128)(2,1)S(1)} %get-tuple-element.2.tl_ref, f32[2,24,128]{2,1,0:T(8,128)S(1)} %broadcast_in_dim.12.rows_ref), custom_call_target="tpu_custom_call" | custom-call | tf_op jit(solution)/shard_map/relaxation/pallas_call | solution.py:367
  (10 shorter events, 0.1 us)
Async XLA Ops:
  0.6 20.5 %copy-start = (s32[256]{0:T(256)S(1)}, s32[256]{0:T(256)}, u32[]{:S(2)}) copy-start(s32[256]{0:T(256)} %order_hbm.1) | copy-start | bytes 3076
  5.8 24.1 %all-to-all-start = ((f32[64,1,1152]{2,1,0:T(1,128)}), f32[64,1,1152]{2,1,0:T(1,128)S(1)}, u32[]{:S(2)}, u32[]{:S(2)}) async-start(f32[64,1,1152]{2,1,0:T(1,128)} %bitcast.6), calls=%async_computation | async-start | bytes 589824 | tf_op jit(solution)/shard_map/all_to_all | solution.py:387

commit v4 on v3

--- a/solution.py
+++ b/solution.py
@@ -33,7 +33,10 @@
 
 LAT_X, LAT_Z = 4, 8
 EXCHANGE = [
-    y * HALF + x * LAT_Z + z for y in range(2) for z in reversed(range(LAT_Z)) for x in range(LAT_X)
+    y * HALF + (k + 2) % LAT_X * LAT_Z + z
+    for y in range(2)
+    for z in reversed(range(LAT_Z))
+    for k in range(LAT_X)
 ]
 
 
@@ -70,7 +73,7 @@
 def synth_kernel(
     order_hbm, log_hbm, geom_hbm, coef_hbm, out_ref,
     order_ref, log_ref, geom_ref, coef_ref, fac_ref, back_ref, leg_ref, coefs_ref, wh_ref, wl_ref, stack_ref,
-    sems,
+    early_ref, sems,
 ):
     lat_pos = lax.axis_index("lat")
     core = lax.axis_index("lon") % 2
@@ -98,7 +101,7 @@
     high = (ORDERS - 1.0) - low
     switch = ORDERS - low
 
-    for c in range(65):
+    def factors(c):
         step = lax.broadcasted_iota(jnp.int32, (8, 128), 0).astype(jnp.float32) + float(8 * c)
         if c < 32:
             order, degree = low, low + step
@@ -114,6 +117,9 @@
         back = jnp.sqrt(jnp.maximum(prior2 - order2, 0.0) / jnp.maximum(4.0 * prior2 - 1.0, 1.0))
         fac_ref[8 * c:8 * c + 8, :] = factor
         back_ref[8 * c:8 * c + 8, :] = jnp.where(prior > order, factor * back, 0.0)
+
+    for c in range(32):
+        factors(c)
 
     copies[1].wait()
     copies[2].wait()
@@ -150,15 +156,12 @@
         return previous * shrink, current * shrink, scaling, jnp.exp(scaling)
 
     zero = jnp.zeros((8, 128), jnp.float32)
-    state = run(0, block_steps, (zero, zero, seed_low, jnp.exp(seed_low)), False, True)
-    state = lax.fori_loop(
-        1, 16, lambda b, st: run(b * block_steps, block_steps, st, False, False), state
-    )
-    state = lax.fori_loop(
-        16, 32, lambda b, st: run(b * block_steps, block_steps, st, True, False), state
-    )
-    run(512, 1, state, True, False)
-
+    state = (zero, zero, seed_low, jnp.exp(seed_low))
+    for b in range(16):
+        state = run(b * block_steps, block_steps, state, False, b == 0)
+        factors(32 + 2 * b)
+        factors(33 + 2 * b)
+    factors(64)
     copies[3].wait()
     for p in range(PAIRS_LOCAL):
         for x in range(2):
@@ -177,7 +180,7 @@
             for side in range(2):
                 for h in range(2):
                     w = parts[h] if side == 0 else parts[h] * (low_sign if h == 0 else high_sign)
-                    at = (((side * PAIRS_LOCAL + p) * 2 + h) * 2 + x) * 8
+                    at = (((h * 2 + side) * PAIRS_LOCAL + p) * 2 + x) * 8
                     wh, wl = split2(w)
                     wh_ref[at:at + 8, :] = wh.astype(jnp.float32)
                     wl_ref[at:at + 8, :] = wl.astype(jnp.float32)
@@ -191,31 +194,50 @@
             column = jnp.broadcast_to(coefs_ref[row:row + 8, 512:513], (8, 128))
             tail = jnp.where(pair_of_lane == p, column, tail)
         tails.append(tail)
-    wh = wh_ref[...].astype(jnp.bfloat16)
-    wl = wl_ref[...].astype(jnp.bfloat16)
-    for t0 in range(0, 8, 2):
+
+    def contract(t0, half):
+        at = 256 * half
         values = jnp.concatenate(
-            [leg_ref[pl.ds(t0 + d, 512, stride=8), :] for d in range(2)], axis=1
+            [leg_ref[pl.ds(8 * at + t0 + d, 256, stride=8), :] for d in range(2)], axis=1
         )
         vh, vl = split2(values)
+        rows = 256 if half == 1 else 128
+        wh = wh_ref[0:rows, at:at + 256].astype(jnp.bfloat16)
+        wl = wl_ref[0:rows, at:at + 256].astype(jnp.bfloat16)
         summed = dot(wh, vh) + dot(wl, vh) + dot(wh, vl)
         for d in range(2):
             t = t0 + d
-            last = leg_ref[pl.ds(512 * 8 + t, 1), :]
             part = summed[:, 128 * d:128 * d + 128]
+            if half == 1:
+                last = leg_ref[pl.ds(512 * 8 + t, 1), :]
             for side in range(2):
-                for h in range(2):
+                for h in range(2 if half == 1 else 1):
                     for x in range(2):
                         picked = None
                         for p in range(PAIRS_LOCAL):
-                            at = (((side * PAIRS_LOCAL + p) * 2 + h) * 2 + x) * 8
-                            block = part[at:at + 8, :]
+                            row = (((h * 2 + side) * PAIRS_LOCAL + p) * 2 + x) * 8
+                            block = part[row:row + 8, :]
                             picked = block if p == 0 else jnp.where(pair_of_lane == p, block, picked)
-                        if h == 1:
+                        q = 2 + (t if side == 0 else 7 - t)
+                        which = (side * 2 + h) * 2 + x
+                        if h == 0:
+                            keep = (side * 2 + x) * 8 + t
+                            if half == 0:
+                                early_ref[keep] = picked
+                                continue
+                            picked = picked + early_ref[keep]
+                        else:
                             term = tails[x] * last
                             picked = picked + (term if side == 0 else term * tail_sign)
-                        q = 2 + (t if side == 0 else 7 - t)
-                        stack_ref[(side * 2 + h) * 2 + x, 6 * q:6 * q + 6, :] = picked[0:6]
+                        stack_ref[which, 6 * q:6 * q + 6, :] = picked[0:6]
+
+    for part in range(4):
+        for b in range(4):
+            state = run((16 + 4 * part + b) * block_steps, block_steps, state, True, False)
+        contract(2 * part, 0)
+    run(512, 1, state, True, False)
+    for part in range(4):
+        contract(2 * part, 1)
 
     unit = lax.broadcasted_iota(jnp.int32, (12, 128), 1) % HALF
     for h in range(2):
@@ -230,7 +252,7 @@
 
     group = lax.broadcasted_iota(jnp.int32, (HALF, 128), 1) // HALF
     wide = lax.broadcasted_iota(jnp.int32, (128, 128), 1)
-    x, z = wide % LAT_X, (wide // LAT_X) % LAT_Z
+    x, z = (wide + 2) % LAT_X, (wide // LAT_X) % LAT_Z
     base = wide // HALF * HALF
     source = [base + x * LAT_Z + (LAT_Z - 1 - z), base + (LAT_X - 1 - x) * LAT_Z + z]
 
@@ -269,6 +291,7 @@
         pltpu.VMEM((256, 512), jnp.float32),
         pltpu.VMEM((256, 512), jnp.float32),
         pltpu.VMEM((8, 72, 128), jnp.float32),
+        pltpu.VMEM((32, 8, 128), jnp.float32),
         pltpu.SemaphoreType.DMA((4,)),
     ]
     return pl.pallas_call(
@@ -391,7 +414,8 @@
     received = lax.all_gather(half, "lon", axis=0, tiled=True, axis_index_groups=cores)
 
     by_pair = pair_orders.reshape(LAT, PAIRS_LOCAL)
-    by_pair = by_pair.reshape(2, LAT_X, LAT_Z, PAIRS_LOCAL)[:, :, ::-1].transpose(3, 0, 2, 1)
+    by_pair = by_pair.reshape(2, LAT_X, LAT_Z, PAIRS_LOCAL)[:, :, ::-1]
+    by_pair = jnp.concatenate([by_pair[:, 2:], by_pair[:, :2]], axis=1).transpose(3, 0, 2, 1)
     by_pair = by_pair.reshape(PAIRS_LOCAL, LAT)
     orders = jnp.stack([by_pair, ORDERS - 1 - by_pair], axis=1)
     orders = jnp.broadcast_to(orders[:, :, None, :], (PAIRS_LOCAL, 2, 2, LAT)).reshape(1, 1024)

time: 37.5 us -> 36.2 us (0.965)
  waiting for transfers between devices: 4.08 us -> 2.22 us
  starting transfers between devices: 15.3 us -> 16.3 us
  Pallas kernels: 7.65 us -> 6.94 us
    all_to_all x1, waiting for transfers between devices: 4.08 us -> 2.22 us  [per_device(): lax.all_to_all(send, 'lat', split_axis=0, concat_axis=0, tiled=True, axis...]
    all_to_all x1, starting transfers between devices: 15.3 us -> 16.3 us  [per_device(): lax.all_to_all(send, 'lat', split_axis=0, concat_axis=0, tiled=True, axis...]
    pallas_call x1, Pallas kernels: 5.15 us -> 4.44 us  [synthesize(): pl.pallas_call(synth_kernel, out_shape=jax.ShapeDtypeStruct((LAT * CHUNKS...]
where the time goes in v4:
time: 36.2 us; the launch traced here: 36 us
  starting transfers between devices  16.3 us (45%)
  Pallas kernels  6.94 us (19%)
  blocking collectives  5 us (14%)
  other arithmetic  4.2 us (12%)
  waiting for transfers between devices  2.22 us (6%)
  between operations  0.76 us (2%)
  local copies, waits for them, and re-layouts  0.59 us (2%)
    all_to_all x1, starting transfers between devices, per_device(): lax.all_to_all(send, 'lat', split_axis=0, concat_axis=0, tiled=True, axis...  16.3 us
    all_gather x1, blocking collectives, per_device(): lax.all_gather(half, 'lon', axis=0, tiled=True, axis_index_groups=cores)  5 us
    pallas_call x1, Pallas kernels, synthesize(): pl.pallas_call(synth_kernel, out_shape=jax.ShapeDtypeStruct((LAT * CHUNKS...  4.44 us
    convert_element_type x1, other arithmetic, per_device(): table_low = (table - rounded).astype(jnp.bfloat16)  4.11 us
    pallas_call x1, Pallas kernels, relax(): pl.pallas_call(relax_kernel, out_shape=(shape, shape), in_specs=[vmem] *...  2.5 us
    all_to_all x1, waiting for transfers between devices, per_device(): lax.all_to_all(send, 'lat', split_axis=0, concat_axis=0, tiled=True, axis...  2.22 us
  transfers between devices with their start and end apart: 1, of which 1 were waited for; matrix products, arithmetic and copies ran while one was open for 13% of the time, Pallas kernels for 0%

profile of v4, /device:TPU:1, one launch (start us, length us, event | category | flops | bytes accessed | tf_op | source)
XLA Modules:
  0.0 36.0 jit_solution(37752459709081924)
XLA Ops:
  0.6 0.0 copy-start
  0.6 4.4 %synthesis.1 = f32[576,128]{1,0:T(8,128)} custom-call(s32[256]{0:T(256)} %order_hbm.1, f32[512]{0:T(512)} %constant.75.clone.log_hbm, f32[2,2,8,128]{3,2,1,0:T(8,128)} %constant.76.clone.geom_hbm, f32[4,2,3,2,513]{4,3,2,1,0:T(2,128)} %coef_hbm.1), custom_call_target="tpu_custom_call" | custom-call | tf_op jit(solution)/shard_map/synthesis/pallas_call | solution.py:297
  5.1 16.3 %all-to-all-start = ((f32[64,1,1152]{2,1,0:T(1,128)}), f32[64,1,1152]{2,1,0:T(1,128)S(1)}, u32[]{:S(2)}, u32[]{:S(2)}) async-start(f32[64,1,1152]{2,1,0:T(1,128)} %bitcast.7), calls=%async_computation | async-start | bytes 589824 | tf_op jit(solution)/shard_map/all_to_all | solution.py:410
  21.5 0.0 copy-done
  21.5 0.1 reshape_reshape.3
  21.7 0.2 copy.9
  21.9 0.1 stack_reshape.3
  22.0 0.1 mul.47
  22.1 4.1 %fusion = (bf16[272,1024]{1,0:T(8,128)(2,1)S(1)}, bf16[272,1024]{1,0:T(8,128)(2,1)S(1)}) fusion(s32[1024]{0:T(1024)S(1)} %fusion.6, s32[272]{0:T(512)S(1)} %iota_add_fusion, s32[1024]{0:T(1024)S(1)} %mul.47), kind=kLoop, calls=%fused_computation.2 | loop fusion | flops 2506752 | bytes 1123392 | tf_op jit(solution)/shard_map/convert_element_type | solution.py:428
  26.2 2.2 %all-to-all-done = f32[64,1,1152]{2,1,0:T(1,128)S(1)} async-done(((f32[64,1,1152]{2,1,0:T(1,128)}), f32[64,1,1152]{2,1,0:T(1,128)S(1)}, u32[]{:S(2)}, u32[]{:S(2)}) %all-to-all-start) | async-done | bytes 294944 | tf_op jit(solution)/shard_map/all_to_all | solution.py:410
  28.5 5.0 %all_gather.3.recv_ref = f32[1152,128]{1,0:T(8,128)S(1)} all-gather(f32[576,128]{1,0:T(8,128)S(1)} %bitcast.6), channel_id=1, replica_groups={{0,1},{2,3},{4,5},{6,7},{8,9},{10,11},{12,13},{14,15},{16,17},{18,19},{..., dimensions={0}, use_global_device_ids=true | all-gather | bytes 884736 | tf_op jit(solution)/shard_map/all_gather | solution.py:414
  33.4 0.1 broadcast_in_dim.12.rows_ref
  33.5 2.5 %relaxation.1 = (f32[3,2,16,256]{3,2,1,0:T(8,128)}, f32[3,2,16,256]{3,2,1,0:T(8,128)}) custom-call(f32[1152,128]{1,0:T(8,128)S(1)} %all_gather.3.recv_ref, bf16[272,1024]{1,0:T(8,128)(2,1)S(1)} %get-tuple-element.5.th_ref, bf16[272,1024]{1,0:T(8,128)(2,1)S(1)} %get-tuple-element.4.tl_ref, f32[2,24,128]{2,1,0:T(8,128)S(1)} %broadcast_in_dim.12.rows_ref), custom_call_target="tpu_custom_call" | custom-call | tf_op jit(solution)/shard_map/relaxation/pallas_call | solution.py:390
  (13 shorter events, 0.1 us)
Async XLA Ops:
  0.6 20.9 %copy-start = (s32[256]{0:T(256)S(1)}, s32[256]{0:T(256)}, u32[]{:S(2)}) copy-start(s32[256]{0:T(256)} %order_hbm.1) | copy-start | bytes 3076
  5.1 23.4 %all-to-all-start = ((f32[64,1,1152]{2,1,0:T(1,128)}), f32[64,1,1152]{2,1,0:T(1,128)S(1)}, u32[]{:S(2)}, u32[]{:S(2)}) async-start(f32[64,1,1152]{2,1,0:T(1,128)} %bitcast.7), calls=%async_computation | async-start | bytes 589824 | tf_op jit(solution)/shard_map/all_to_all | solution.py:410

commit v5 on v4

--- a/solution.py
+++ b/solution.py
@@ -115,6 +115,8 @@
         prior2 = prior * prior
         factor = jnp.sqrt(jnp.maximum(4.0 * degree2 - 1.0, 1.0) / jnp.maximum(degree2 - order2, 1.0))
         back = jnp.sqrt(jnp.maximum(prior2 - order2, 0.0) / jnp.maximum(4.0 * prior2 - 1.0, 1.0))
+        if c >= 32:
+            factor = jnp.where(degree > order, factor, 0.0)
         fac_ref[8 * c:8 * c + 8, :] = factor
         back_ref[8 * c:8 * c + 8, :] = jnp.where(prior > order, factor * back, 0.0)
 
@@ -138,15 +140,16 @@
             s = base + k
             fac = fac_ref[pl.ds(s, 1), :]
             back = back_ref[pl.ds(s, 1), :]
-            if first and k == 0:
+            from_previous = back * previous
+            if restart:
+                starting = switch == (s.astype(jnp.float32) if not isinstance(s, int) else float(s))
+                scaling = jnp.where(starting, seed_high, scaling)
+                scale = jnp.where(starting, start_scale, scale)
+                value = (fac * cosine) * current + (jnp.where(starting, 1.0, 0.0) - from_previous)
+            elif first and k == 0:
                 value = jnp.ones((8, 128), jnp.float32)
             else:
-                value = (fac * cosine) * current - back * previous
-            if restart:
-                starting = switch == (s.astype(jnp.float32) if not isinstance(s, int) else float(s))
-                value = jnp.where(starting, 1.0, value)
-                scaling = jnp.where(starting, seed_high, scaling)
-                scale = jnp.where(starting, start_scale, scale)
+                value = (fac * cosine) * current - from_previous
             previous, current = current, value
             at = s * 8 if isinstance(s, int) else pl.multiple_of(s * 8, 8)
             leg_ref[pl.ds(at, 8), :] = value * scale
@@ -305,29 +308,43 @@
     )(pair_orders, norm_logs(), geometry(), coefficients)
 
 
-def relax_kernel(recv_ref, th_ref, tl_ref, rows_ref, pot_ref, mag_ref, dh_ref, dl_ref, turn_ref, plane_ref):
+def relax_kernel(
+    recv_ref, th_ref, tl_ref, rows_ref, pot_hbm, mag_hbm, dh_ref, dl_ref, turn_ref, plane_ref, pot_ref, mag_ref, sems
+):
     lane = lax.broadcasted_iota(jnp.int32, (LAT, 128), 1)
     for half in range(2):
         start = half * LAT * CHUNKS
         at = half * 128
         rest = recv_ref[pl.ds(start + 8, LAT, stride=CHUNKS), :]
+        crossed = pltpu.roll(rest, 64, 1)
         for both in range(8):
             main = recv_ref[pl.ds(start + both, LAT, stride=CHUNKS), :]
             for x in range(2):
                 ox = both * 2 + x
-                head = pltpu.roll(main, 64, 1) if x else main
-                shift = (64 - 8 * ox) % 128
-                tail = pltpu.roll(rest, shift, 1) if shift else rest
-                high, low = split2(jnp.where(lane < 64, head, tail))
-                dh_ref[ox * LAT:ox * LAT + LAT, at:at + 128] = high
-                dl_ref[ox * LAT:ox * LAT + LAT, at:at + 128] = low
-    dh, dl = dh_ref[...], dl_ref[...]
-    th, tl = th_ref[...], tl_ref[...]
-    turn_ref[0:COLS, :] = dot(th, dh) + dot(tl, dh) + dot(th, dl)
+                side = 1 - x
+                tail = rest if (ox >= 8) == (side == 1) else crossed
+                tail = jnp.where(lane // 8 == side * 8 + ox % 8, tail, 0.0)
+                value = jnp.where(lane < 64, main, tail) if x == 0 else jnp.where(lane < 64, tail, main)
+                high, low = split2(value)
+                row = (x * 8 + both) * LAT
+                dh_ref[row:row + LAT, at:at + 128] = high
+                dl_ref[row:row + LAT, at:at + 128] = low
+    parts = []
+    for x in range(2):
+        k = slice(512 * x, 512 * x + 512)
+        dh, dl, th, tl = dh_ref[k, :], dl_ref[k, :], th_ref[:, k], tl_ref[:, k]
+        parts.append(dot(th, dh) + dot(tl, dh) + dot(th, dl))
+    for half in range(2):
+        block = slice(128 * half, 128 * half + 128)
+        turn_ref[0:COLS, block] = parts[0][:, block] + pltpu.roll(parts[1][:, block], 64, 1)
     turn_ref[COLS:, :] = jnp.zeros((384 - COLS, 256), jnp.float32)
     for j in range(3):
         for half in range(2):
             turned = turn_ref[128 * j:128 * j + 128, 128 * half:128 * half + 128].T
+            tail = turned[64:72, :]
+            for g in range(1, 8):
+                tail = tail + turned[64 + 8 * g:72 + 8 * g, :]
+            turned = jnp.concatenate([turned[0:64, :], tail], axis=0)
             starts = [2 - 2 * half] + [HALO + r for r in own_rows(half)[::2]] + [20 + 2 * half]
             for k, e in enumerate(starts):
                 plane_ref[j, 6 * e:6 * e + 12, :] = turned[12 * k:12 * k + 12, :]
@@ -360,9 +377,19 @@
     def cross(a, b):
         return [a[1] * b[2] - a[2] * b[1], a[2] * b[0] - a[0] * b[2], a[0] * b[1] - a[1] * b[0]]
 
-    magnetic = None
-    for _ in range(STEPS):
+    def centre(a):
+        a = pltpu.roll(pltpu.roll(a, EXT - HALO, 0), 384 - HALO, 1)
+        return a[0:BAND, 0:SECTOR]
+
+    pot_copy = pltpu.make_async_copy(pot_ref, pot_hbm, sems.at[0])
+    mag_copy = pltpu.make_async_copy(mag_ref, mag_hbm, sems.at[1])
+    for step in range(STEPS):
         magnetic = [[jnp.where(inside, b, 0.0) for b in pair] for pair in curl(field)]
+        if step == STEPS - 1:
+            for c in range(3):
+                for r in range(2):
+                    mag_ref[c, r] = centre(magnetic[c][r])
+            mag_copy.start()
         current = curl(magnetic)
         for r in range(2):
             b = [magnetic[c][r] for c in range(3)]
@@ -373,30 +400,31 @@
             for c in range(3):
                 moved = field[c][r] + time_step * (push[c] - resist * j[c])
                 field[c][r] = jnp.where(inside, moved, 0.0)
-
-    def centre(a):
-        a = pltpu.roll(pltpu.roll(a, EXT - HALO, 0), 384 - HALO, 1)
-        return a[0:BAND, 0:SECTOR]
-
     for c in range(3):
         for r in range(2):
             pot_ref[c, r] = centre(field[c][r])
-            mag_ref[c, r] = centre(magnetic[c][r])
+    pot_copy.start()
+    mag_copy.wait()
+    pot_copy.wait()
 
 
 def relax(received, table_high, table_low, rows):
     shape = jax.ShapeDtypeStruct((3, 2, BAND, SECTOR), jnp.float32)
     vmem = pl.BlockSpec(memory_space=pltpu.VMEM)
+    hbm = pl.BlockSpec(memory_space=pltpu.HBM)
     return pl.pallas_call(
         relax_kernel,
         out_shape=(shape, shape),
         in_specs=[vmem] * 4,
-        out_specs=(vmem, vmem),
+        out_specs=(hbm, hbm),
         scratch_shapes=[
             pltpu.VMEM((1024, 256), jnp.bfloat16),
             pltpu.VMEM((1024, 256), jnp.bfloat16),
             pltpu.VMEM((384, 256), jnp.float32),
             pltpu.VMEM((3, 144, 128), jnp.float32),
+            pltpu.VMEM((3, 2, BAND, SECTOR), jnp.float32),
+            pltpu.VMEM((3, 2, BAND, SECTOR), jnp.float32),
+            pltpu.SemaphoreType.DMA((2,)),
         ],
         compiler_params=pltpu.CompilerParams(vmem_limit_bytes=40 * 1024 * 1024),
         name="relaxation",
@@ -417,9 +445,9 @@
     by_pair = by_pair.reshape(2, LAT_X, LAT_Z, PAIRS_LOCAL)[:, :, ::-1]
     by_pair = jnp.concatenate([by_pair[:, 2:], by_pair[:, :2]], axis=1).transpose(3, 0, 2, 1)
     by_pair = by_pair.reshape(PAIRS_LOCAL, LAT)
-    orders = jnp.stack([by_pair, ORDERS - 1 - by_pair], axis=1)
-    orders = jnp.broadcast_to(orders[:, :, None, :], (PAIRS_LOCAL, 2, 2, LAT)).reshape(1, 1024)
-    is_cos = (jnp.arange(1024, dtype=jnp.int32)[None, :] // LAT) % 2 == 0
+    orders = jnp.stack([by_pair, ORDERS - 1 - by_pair], axis=1).reshape(1, 512)
+    orders = jnp.concatenate([orders, orders], axis=1)
+    is_cos = jnp.arange(1024, dtype=jnp.int32)[None, :] < 512
     columns = lon_pos * SECTOR - HALO + jnp.arange(COLS, dtype=jnp.int32)[:, None]
     turns = (orders * columns + jnp.where(is_cos, NP // 4, 0)) & (NP - 1)
     table = jnp.sin(turns.astype(jnp.float32) * (2.0 * math.pi / NP))

time: 36.2 us -> 35.9 us (level)
  no operation moved by 1% of the time
where the time goes in v5:
time: 35.9 us; the launch traced here: 35.7 us
  starting transfers between devices  16.3 us (45%)
  Pallas kernels  6.61 us (18%)
  blocking collectives  5 us (14%)
  other arithmetic  4.2 us (12%)
  waiting for transfers between devices  2.22 us (6%)
  between operations  0.76 us (2%)
  local copies, waits for them, and re-layouts  0.59 us (2%)
    all_to_all x1, starting transfers between devices, per_device(): lax.all_to_all(send, 'lat', split_axis=0, concat_axis=0, tiled=True, axis...  16.3 us
    all_gather x1, blocking collectives, per_device(): lax.all_gather(half, 'lon', axis=0, tiled=True, axis_index_groups=cores)  5 us
    pallas_call x1, Pallas kernels, synthesize(): pl.pallas_call(synth_kernel, out_shape=jax.ShapeDtypeStruct((LAT * CHUNKS...  4.34 us
    convert_element_type x1, other arithmetic, per_device(): table_low = (table - rounded).astype(jnp.bfloat16)  4.11 us
    pallas_call x1, Pallas kernels, relax(): pl.pallas_call(relax_kernel, out_shape=(shape, shape), in_specs=[vmem] *...  2.26 us
    all_to_all x1, waiting for transfers between devices, per_device(): lax.all_to_all(send, 'lat', split_axis=0, concat_axis=0, tiled=True, axis...  2.22 us
  transfers between devices with their start and end apart: 1, of which 1 were waited for; matrix products, arithmetic and copies ran while one was open for 13% of the time, Pallas kernels for 0%

profile of v5, /device:TPU:1, one launch (start us, length us, event | category | flops | bytes accessed | tf_op | source)
XLA Modules:
  0.0 35.7 jit_solution(10264564828190395663)
XLA Ops:
  0.6 0.0 copy-start
  0.6 4.3 %synthesis.1 = f32[576,128]{1,0:T(8,128)} custom-call(s32[256]{0:T(256)} %order_hbm.1, f32[512]{0:T(512)} %constant.45.clone.log_hbm, f32[2,2,8,128]{3,2,1,0:T(8,128)} %constant.46.clone.geom_hbm, f32[4,2,3,2,513]{4,3,2,1,0:T(2,128)} %coef_hbm.1), custom_call_target="tpu_custom_call" | custom-call | tf_op jit(solution)/shard_map/synthesis/pallas_call | solution.py:300
  5.0 16.3 %all-to-all-start = ((f32[64,1,1152]{2,1,0:T(1,128)}), f32[64,1,1152]{2,1,0:T(1,128)S(1)}, u32[]{:S(2)}, u32[]{:S(2)}) async-start(f32[64,1,1152]{2,1,0:T(1,128)} %bitcast.8), calls=%async_computation | async-start | bytes 589824 | tf_op jit(solution)/shard_map/all_to_all | solution.py:438
  21.4 0.0 copy-done
  21.4 0.1 reshape_reshape.3
  21.6 0.2 copy.10
  21.8 0.1 stack_reshape.3
  21.9 0.1 reshape.80
  22.0 4.1 %fusion = (bf16[272,1024]{1,0:T(8,128)(2,1)S(1)}, bf16[272,1024]{1,0:T(8,128)(2,1)S(1)}) fusion(s32[1024]{0:T(1024)S(1)} %fusion.1, s32[272]{0:T(512)S(1)} %iota_add_fusion, s32[1024]{0:T(1024)S(1)} %bitcast.9), kind=kLoop, calls=%fused_computation.2 | loop fusion | flops 2506752 | bytes 1123392 | tf_op jit(solution)/shard_map/convert_element_type | solution.py:456
  26.1 2.2 %all-to-all-done = f32[64,1,1152]{2,1,0:T(1,128)S(1)} async-done(((f32[64,1,1152]{2,1,0:T(1,128)}), f32[64,1,1152]{2,1,0:T(1,128)S(1)}, u32[]{:S(2)}, u32[]{:S(2)}) %all-to-all-start) | async-done | bytes 294944 | tf_op jit(solution)/shard_map/all_to_all | solution.py:438
  28.4 5.0 %all_gather.3.recv_ref = f32[1152,128]{1,0:T(8,128)S(1)} all-gather(f32[576,128]{1,0:T(8,128)S(1)} %bitcast.7), channel_id=1, replica_groups={{0,1},{2,3},{4,5},{6,7},{8,9},{10,11},{12,13},{14,15},{16,17},{18,19},{..., dimensions={0}, use_global_device_ids=true | all-gather | bytes 884736 | tf_op jit(solution)/shard_map/all_gather | solution.py:442
  33.3 0.1 broadcast_in_dim.9.rows_ref
  33.4 2.3 %relaxation.1 = (f32[3,2,16,256]{3,2,1,0:T(8,128)}, f32[3,2,16,256]{3,2,1,0:T(8,128)}) custom-call(f32[1152,128]{1,0:T(8,128)S(1)} %all_gather.3.recv_ref, bf16[272,1024]{1,0:T(8,128)(2,1)S(1)} %get-tuple-element.5.th_ref, bf16[272,1024]{1,0:T(8,128)(2,1)S(1)} %get-tuple-element.4.tl_ref, f32[2,24,128]{2,1,0:T(8,128)S(1)} %broadcast_in_dim.9.rows_ref), custom_call_target="tpu_custom_call" | custom-call | tf_op jit(solution)/shard_map/relaxation/pallas_call | solution.py:415
  (13 shorter events, 0.1 us)
Async XLA Ops:
  0.6 20.8 %copy-start = (s32[256]{0:T(256)S(1)}, s32[256]{0:T(256)}, u32[]{:S(2)}) copy-start(s32[256]{0:T(256)} %order_hbm.1) | copy-start | bytes 3076
  5.0 23.4 %all-to-all-start = ((f32[64,1,1152]{2,1,0:T(1,128)}), f32[64,1,1152]{2,1,0:T(1,128)S(1)}, u32[]{:S(2)}, u32[]{:S(2)}) async-start(f32[64,1,1152]{2,1,0:T(1,128)} %bitcast.8), calls=%async_computation | async-start | bytes 589824 | tf_op jit(solution)/shard_map/all_to_all | solution.py:438

commit v6 on v5

--- a/solution.py
+++ b/solution.py
@@ -336,8 +336,10 @@
         parts.append(dot(th, dh) + dot(tl, dh) + dot(th, dl))
     for half in range(2):
         block = slice(128 * half, 128 * half + 128)
-        turn_ref[0:COLS, block] = parts[0][:, block] + pltpu.roll(parts[1][:, block], 64, 1)
-    turn_ref[COLS:, :] = jnp.zeros((384 - COLS, 256), jnp.float32)
+        summed = parts[0][:, block] + pltpu.roll(parts[1][:, block], 64, 1)
+        turn_ref[0:COLS - 8, block] = summed[0:COLS - 8]
+        turn_ref[376:384, block] = summed[COLS - 8:COLS]
+    turn_ref[COLS - 8:376, :] = jnp.zeros((384 - COLS, 256), jnp.float32)
     for j in range(3):
         for half in range(2):
             turned = turn_ref[128 * j:128 * j + 128, 128 * half:128 * half + 128].T
@@ -378,8 +380,7 @@
         return [a[1] * b[2] - a[2] * b[1], a[2] * b[0] - a[0] * b[2], a[0] * b[1] - a[1] * b[0]]
 
     def centre(a):
-        a = pltpu.roll(pltpu.roll(a, EXT - HALO, 0), 384 - HALO, 1)
-        return a[0:BAND, 0:SECTOR]
+        return pltpu.roll(a[:, 0:SECTOR], EXT - HALO, 0)[0:BAND]
 
     pot_copy = pltpu.make_async_copy(pot_ref, pot_hbm, sems.at[0])
     mag_copy = pltpu.make_async_copy(mag_ref, mag_hbm, sems.at[1])
@@ -448,7 +449,8 @@
     orders = jnp.stack([by_pair, ORDERS - 1 - by_pair], axis=1).reshape(1, 512)
     orders = jnp.concatenate([orders, orders], axis=1)
     is_cos = jnp.arange(1024, dtype=jnp.int32)[None, :] < 512
-    columns = lon_pos * SECTOR - HALO + jnp.arange(COLS, dtype=jnp.int32)[:, None]
+    columns = jnp.arange(COLS, dtype=jnp.int32)[:, None]
+    columns = lon_pos * SECTOR + jnp.where(columns < COLS - 8, columns, columns - COLS)
     turns = (orders * columns + jnp.where(is_cos, NP // 4, 0)) & (NP - 1)
     table = jnp.sin(turns.astype(jnp.float32) * (2.0 * math.pi / NP))
     rounded = lax.reduce_precision(table, exponent_bits=8, mantissa_bits=7)

time: 35.9 us -> 35.7 us (level)
  no operation moved by 1% of the time
where the time goes in v6:
time: 35.7 us; the launch traced here: 35.6 us
  starting transfers between devices  16.3 us (46%)
  Pallas kernels  6.48 us (18%)
  blocking collectives  5 us (14%)
  other arithmetic  4.2 us (12%)
  waiting for transfers between devices  2.22 us (6%)
  between operations  0.76 us (2%)
  local copies, waits for them, and re-layouts  0.59 us (2%)
    all_to_all x1, starting transfers between devices, per_device(): lax.all_to_all(send, 'lat', split_axis=0, concat_axis=0, tiled=True, axis...  16.3 us
    all_gather x1, blocking collectives, per_device(): lax.all_gather(half, 'lon', axis=0, tiled=True, axis_index_groups=cores)  5 us
    pallas_call x1, Pallas kernels, synthesize(): pl.pallas_call(synth_kernel, out_shape=jax.ShapeDtypeStruct((LAT * CHUNKS...  4.34 us
    convert_element_type x1, other arithmetic, per_device(): table_low = (table - rounded).astype(jnp.bfloat16)  4.11 us
    all_to_all x1, waiting for transfers between devices, per_device(): lax.all_to_all(send, 'lat', split_axis=0, concat_axis=0, tiled=True, axis...  2.22 us
    pallas_call x1, Pallas kernels, relax(): pl.pallas_call(relax_kernel, out_shape=(shape, shape), in_specs=[vmem] *...  2.14 us
  transfers between devices with their start and end apart: 1, of which 1 were waited for; matrix products, arithmetic and copies ran while one was open for 13% of the time, Pallas kernels for 0%

profile of v6, /device:TPU:1, one launch (start us, length us, event | category | flops | bytes accessed | tf_op | source)
XLA Modules:
  0.0 35.6 jit_solution(2119627169066039896)
XLA Ops:
  0.6 0.0 copy-start
  0.6 4.3 %synthesis.1 = f32[576,128]{1,0:T(8,128)} custom-call(s32[256]{0:T(256)} %order_hbm.1, f32[512]{0:T(512)} %constant.49.clone.log_hbm, f32[2,2,8,128]{3,2,1,0:T(8,128)} %constant.50.clone.geom_hbm, f32[4,2,3,2,513]{4,3,2,1,0:T(2,128)} %coef_hbm.1), custom_call_target="tpu_custom_call" | custom-call | tf_op jit(solution)/shard_map/synthesis/pallas_call | solution.py:300
  5.0 16.3 %all-to-all-start = ((f32[64,1,1152]{2,1,0:T(1,128)}), f32[64,1,1152]{2,1,0:T(1,128)S(1)}, u32[]{:S(2)}, u32[]{:S(2)}) async-start(f32[64,1,1152]{2,1,0:T(1,128)} %bitcast.8), calls=%async_computation | async-start | bytes 589824 | tf_op jit(solution)/shard_map/all_to_all | solution.py:439
  21.4 0.0 copy-done
  21.4 0.1 reshape_reshape.3
  21.6 0.2 copy.10
  21.8 0.1 stack_reshape.3
  21.9 0.1 reshape.90
  22.0 4.1 %fusion = (bf16[272,1024]{1,0:T(8,128)(2,1)S(1)}, bf16[272,1024]{1,0:T(8,128)(2,1)S(1)}) fusion(s32[1024]{0:T(1024)S(1)} %fusion.1, s32[272]{0:T(512)S(1)} %fusion.2, s32[1024]{0:T(1024)S(1)} %bitcast.9), kind=kLoop, calls=%fused_computation.2 | loop fusion | flops 2506752 | bytes 1123392 | tf_op jit(solution)/shard_map/convert_element_type | solution.py:458
  26.1 2.2 %all-to-all-done = f32[64,1,1152]{2,1,0:T(1,128)S(1)} async-done(((f32[64,1,1152]{2,1,0:T(1,128)}), f32[64,1,1152]{2,1,0:T(1,128)S(1)}, u32[]{:S(2)}, u32[]{:S(2)}) %all-to-all-start) | async-done | bytes 294944 | tf_op jit(solution)/shard_map/all_to_all | solution.py:439
  28.4 5.0 %all_gather.3.recv_ref = f32[1152,128]{1,0:T(8,128)S(1)} all-gather(f32[576,128]{1,0:T(8,128)S(1)} %bitcast.7), channel_id=1, replica_groups={{0,1},{2,3},{4,5},{6,7},{8,9},{10,11},{12,13},{14,15},{16,17},{18,19},{..., dimensions={0}, use_global_device_ids=true | all-gather | bytes 884736 | tf_op jit(solution)/shard_map/all_gather | solution.py:443
  33.3 0.1 broadcast_in_dim.9.rows_ref
  33.4 2.1 %relaxation.1 = (f32[3,2,16,256]{3,2,1,0:T(8,128)}, f32[3,2,16,256]{3,2,1,0:T(8,128)}) custom-call(f32[1152,128]{1,0:T(8,128)S(1)} %all_gather.3.recv_ref, bf16[272,1024]{1,0:T(8,128)(2,1)S(1)} %get-tuple-element.5.th_ref, bf16[272,1024]{1,0:T(8,128)(2,1)S(1)} %get-tuple-element.4.tl_ref, f32[2,24,128]{2,1,0:T(8,128)S(1)} %broadcast_in_dim.9.rows_ref), custom_call_target="tpu_custom_call" | custom-call | tf_op jit(solution)/shard_map/relaxation/pallas_call | solution.py:416
  (13 shorter events, 0.1 us)
Async XLA Ops:
  0.6 20.8 %copy-start = (s32[256]{0:T(256)S(1)}, s32[256]{0:T(256)}, u32[]{:S(2)}) copy-start(s32[256]{0:T(256)} %order_hbm.1) | copy-start | bytes 3076
  5.0 23.4 %all-to-all-start = ((f32[64,1,1152]{2,1,0:T(1,128)}), f32[64,1,1152]{2,1,0:T(1,128)S(1)}, u32[]{:S(2)}, u32[]{:S(2)}) async-start(f32[64,1,1152]{2,1,0:T(1,128)} %bitcast.8), calls=%async_computation | async-start | bytes 589824 | tf_op jit(solution)/shard_map/all_to_all | solution.py:439

commit v7 on v6

--- a/solution.py
+++ b/solution.py
@@ -309,7 +309,7 @@
 
 
 def relax_kernel(
-    recv_ref, th_ref, tl_ref, rows_ref, pot_hbm, mag_hbm, dh_ref, dl_ref, turn_ref, plane_ref, pot_ref, mag_ref, sems
+    recv_ref, th_ref, tl_ref, pot_hbm, mag_hbm, dh_ref, dl_ref, turn_ref, plane_ref, pot_ref, mag_ref, sems
 ):
     lane = lax.broadcasted_iota(jnp.int32, (LAT, 128), 1)
     for half in range(2):
@@ -355,8 +355,11 @@
         for cr in range(6)
     ]
     field = [[planes[c * 2 + r] for r in range(2)] for c in range(3)]
-    scale = jnp.concatenate([rows_ref[0]] * 3, axis=1)
-    inside = jnp.concatenate([rows_ref[1]] * 3, axis=1) > 0.5
+    row_ids = lax.broadcasted_iota(jnp.int32, (EXT, 128), 0) + (lax.axis_index("lat") * BAND - HALO)
+    theta = span_start + (row_ids.astype(jnp.float32) + 0.5) * (span_width / NT)
+    scale = jnp.concatenate([1.0 / (2.0 * (3.0 * NT / NP) * jnp.sin(theta))] * 3, axis=1)
+    row_ids = jnp.concatenate([row_ids] * 3, axis=1)
+    inside = (row_ids >= 0) & (row_ids < NT)
 
     def d_theta(a):
         return 0.5 * (pltpu.roll(a, EXT - 1, 0) - pltpu.roll(a, 1, 0))
@@ -409,14 +412,14 @@
     pot_copy.wait()
 
 
-def relax(received, table_high, table_low, rows):
+def relax(received, table_high, table_low):
     shape = jax.ShapeDtypeStruct((3, 2, BAND, SECTOR), jnp.float32)
     vmem = pl.BlockSpec(memory_space=pltpu.VMEM)
     hbm = pl.BlockSpec(memory_space=pltpu.HBM)
     return pl.pallas_call(
         relax_kernel,
         out_shape=(shape, shape),
-        in_specs=[vmem] * 4,
+        in_specs=[vmem] * 3,
         out_specs=(hbm, hbm),
         scratch_shapes=[
             pltpu.VMEM((1024, 256), jnp.bfloat16),
@@ -429,11 +432,10 @@
         ],
         compiler_params=pltpu.CompilerParams(vmem_limit_bytes=40 * 1024 * 1024),
         name="relaxation",
-    )(received, table_high, table_low, rows)
+    )(received, table_high, table_low)
 
 
 def per_device(coefficients, pair_orders):
-    lat_pos = lax.axis_index("lat")
     lon_pos = lax.axis_index("lon")
     send = synthesize(pair_orders, coefficients).reshape(LAT, 1, CHUNKS * 128)
     half = lax.all_to_all(
@@ -457,12 +459,7 @@
     table_high = rounded.astype(jnp.bfloat16)
     table_low = (table - rounded).astype(jnp.bfloat16)
 
-    row_ids = lat_pos * BAND - HALO + jnp.arange(EXT, dtype=jnp.int32)
-    theta = span_start + (row_ids.astype(jnp.float32) + 0.5) * (span_width / NT)
-    scale = 1.0 / (2.0 * (3.0 * NT / NP) * jnp.sin(theta))
-    inside = ((row_ids >= 0) & (row_ids < NT)).astype(jnp.float32)
-    rows = jnp.broadcast_to(jnp.stack([scale, inside])[:, :, None], (2, EXT, 128))
-    return relax(received, table_high, table_low, rows)
+    return relax(received, table_high, table_low)
 
 
 def solution(mesh):

time: 35.7 us -> 35.7 us (level)
  no operation moved by 1% of the time
where the time goes in v7:
time: 35.7 us; the launch traced here: 35.5 us
  starting transfers between devices  16.3 us (46%)
  Pallas kernels  6.51 us (18%)
  blocking collectives  5 us (14%)
  other arithmetic  4.14 us (12%)
  waiting for transfers between devices  2.31 us (6%)
  between operations  0.73 us (2%)
  local copies, waits for them, and re-layouts  0.51 us (1%)
    all_to_all x1, starting transfers between devices, per_device(): lax.all_to_all(send, 'lat', split_axis=0, concat_axis=0, tiled=True, axis...  16.3 us
    all_gather x1, blocking collectives, per_device(): lax.all_gather(half, 'lon', axis=0, tiled=True, axis_index_groups=cores)  5 us
    pallas_call x1, Pallas kernels, synthesize(): pl.pallas_call(synth_kernel, out_shape=jax.ShapeDtypeStruct((LAT * CHUNKS...  4.34 us
    convert_element_type x1, other arithmetic, per_device(): table_low = (table - rounded).astype(jnp.bfloat16)  4.11 us
    all_to_all x1, waiting for transfers between devices, per_device(): lax.all_to_all(send, 'lat', split_axis=0, concat_axis=0, tiled=True, axis...  2.31 us
    pallas_call x1, Pallas kernels, relax(): pl.pallas_call(relax_kernel, out_shape=(shape, shape), in_specs=[vmem] *...  2.17 us
  transfers between devices with their start and end apart: 1, of which 1 were waited for; matrix products, arithmetic and copies ran while one was open for 13% of the time, Pallas kernels for 0%

profile of v7, /device:TPU:1, one launch (start us, length us, event | category | flops | bytes accessed | tf_op | source)
XLA Modules:
  0.0 35.5 jit_solution(15471131546667745783)
XLA Ops:
  0.6 0.0 copy-start
  0.6 4.3 %synthesis.1 = f32[576,128]{1,0:T(8,128)} custom-call(s32[256]{0:T(256)} %order_hbm.1, f32[512]{0:T(512)} %constant.26.clone.log_hbm, f32[2,2,8,128]{3,2,1,0:T(8,128)} %constant.27.clone.geom_hbm, f32[4,2,3,2,513]{4,3,2,1,0:T(2,128)} %coef_hbm.1), custom_call_target="tpu_custom_call" | custom-call | tf_op jit(solution)/shard_map/synthesis/pallas_call | solution.py:300
  5.0 16.3 %all-to-all-start = ((f32[64,1,1152]{2,1,0:T(1,128)}), f32[64,1,1152]{2,1,0:T(1,128)S(1)}, u32[]{:S(2)}, u32[]{:S(2)}) async-start(f32[64,1,1152]{2,1,0:T(1,128)} %bitcast.8), calls=%async_computation | async-start | bytes 589824 | tf_op jit(solution)/shard_map/all_to_all | solution.py:441
  21.3 0.0 copy-done
  21.3 0.1 reshape_reshape.3
  21.5 0.2 copy.10
  21.7 0.1 stack_reshape.3
  21.8 0.1 reshape.48
  21.9 4.1 %fusion = (bf16[272,1024]{1,0:T(8,128)(2,1)S(1)}, bf16[272,1024]{1,0:T(8,128)(2,1)S(1)}) fusion(s32[1024]{0:T(1024)S(1)} %fusion.1, s32[272]{0:T(512)S(1)} %fusion.2, s32[1024]{0:T(1024)S(1)} %bitcast.9), kind=kLoop, calls=%fused_computation.2 | loop fusion | flops 2506752 | bytes 1123392 | tf_op jit(solution)/shard_map/convert_element_type | solution.py:460
  26.0 2.3 %all-to-all-done = f32[64,1,1152]{2,1,0:T(1,128)S(1)} async-done(((f32[64,1,1152]{2,1,0:T(1,128)}), f32[64,1,1152]{2,1,0:T(1,128)S(1)}, u32[]{:S(2)}, u32[]{:S(2)}) %all-to-all-start) | async-done | bytes 294944 | tf_op jit(solution)/shard_map/all_to_all | solution.py:441
  28.4 5.0 %all_gather.3.recv_ref = f32[1152,128]{1,0:T(8,128)S(1)} all-gather(f32[576,128]{1,0:T(8,128)S(1)} %bitcast.7), channel_id=1, replica_groups={{0,1},{2,3},{4,5},{6,7},{8,9},{10,11},{12,13},{14,15},{16,17},{18,19},{..., dimensions={0}, use_global_device_ids=true | all-gather | bytes 884736 | tf_op jit(solution)/shard_map/all_gather | solution.py:445
  33.3 2.2 %relaxation.1 = (f32[3,2,16,256]{3,2,1,0:T(8,128)}, f32[3,2,16,256]{3,2,1,0:T(8,128)}) custom-call(f32[1152,128]{1,0:T(8,128)S(1)} %all_gather.3.recv_ref, bf16[272,1024]{1,0:T(8,128)(2,1)S(1)} %get-tuple-element.5.th_ref, bf16[272,1024]{1,0:T(8,128)(2,1)S(1)} %get-tuple-element.4.tl_ref), custom_call_target="tpu_custom_call" | custom-call | tf_op jit(solution)/shard_map/relaxation/pallas_call | solution.py:419
  (10 shorter events, 0.1 us)
Async XLA Ops:
  0.6 20.7 %copy-start = (s32[256]{0:T(256)S(1)}, s32[256]{0:T(256)}, u32[]{:S(2)}) copy-start(s32[256]{0:T(256)} %order_hbm.1) | copy-start | bytes 3076
  5.0 23.4 %all-to-all-start = ((f32[64,1,1152]{2,1,0:T(1,128)}), f32[64,1,1152]{2,1,0:T(1,128)S(1)}, u32[]{:S(2)}, u32[]{:S(2)}) async-start(f32[64,1,1152]{2,1,0:T(1,128)} %bitcast.8), calls=%async_computation | async-start | bytes 589824 | tf_op jit(solution)/shard_map/all_to_all | solution.py:441
